TPU v7x, 32 devices: a whole 2x2x4 slice. The times are simulated.
32 devices in a mesh: wide: 8 (over z, core), narrow: 4 (over y, x).
Axes of the slice: x: 2, y: 2, z: 4, core: 2. Of those that a mesh axis runs over, the one named last changes fastest.
Arguments:
- tokens: bfloat16 [8192, 2304], P(('wide', 'narrow')), may hold values from -6 to 6
- target: bfloat16 [8192, 2304], P(('wide', 'narrow')), may hold values from -6 to 6
- combine: bfloat16 [8192], P(('wide', 'narrow')), may hold values from 0.25 to 1
- filled: int32 [8], P('wide'), may hold values from 512 to 1024, as said below
- w_gate: bfloat16 [2304, 2048], P(None, 'narrow'), may hold values from -0.125 to 0.125
- w_up: bfloat16 [2304, 2048], P(None, 'narrow'), may hold values from -0.125 to 0.125
- w_down: bfloat16 [2048, 2304], P('narrow'), may hold values from -0.125 to 0.125
- momentum: float32 [8, 2048, 2304], P('wide', 'narrow'), may hold values from -6 to 6
Outputs:
- momentum_out: float32 [8, 2048, 2304], P('wide', 'narrow')
- update: bfloat16 [2048, 2304], P('narrow')
Inputs may be any that keep to these rules, and one draw needn't show every extreme that they name: `filled`: rows of a replica at or after its count are empty buffer slots; some replica's buffer is full in every draw.
All inputs are finite; a program needn't handle non-finite values.
Results may differ from a plain program's by a relative error of at most 0.015.
Values may be sent and summed in bfloat16 or wider, within the bound.
A program may use at most 128 MiB of HBM per device.

v0:
```python
import functools
import math

import jax
import jax.numpy as jnp
import numpy as np
from jax import lax
from jax.experimental import pallas as pl
from jax.experimental.pallas import tpu as pltpu
from jax.sharding import PartitionSpec as P

SPAN = 64
BAND = 16
TILE = 256
BF = jnp.bfloat16
F32 = jnp.float32


def block_table(blocks):
    row = np.arange(blocks * BAND)[:, None]
    col = np.arange(blocks * SPAN)[None, :]
    factor = np.where(row % BAND == 0, math.sqrt(1.0 / SPAN), math.sqrt(2.0 / SPAN))
    value = factor * np.cos(math.pi * (2.0 * (col % SPAN) + 1.0) * (row % BAND) / (2.0 * SPAN))
    return np.where(row // BAND == col // SPAN, value, 0.0).astype(np.float32)


def halves(value):
    high = value.astype(BF)
    return high, (value - high.astype(F32)).astype(BF)


def dot3(left, right, contract):
    dims = (((contract[0],), (contract[1],)), ((), ()))
    dot = functools.partial(lax.dot_general, dimension_numbers=dims, preferred_element_type=F32)
    return dot(left[0], right[0]) + (dot(left[1], right[0]) + dot(left[0], right[1]))


def decode_tile(band, tables):
    wide = dot3(halves(band), tables[3], (1, 0))
    return dot3(tables[1], halves(wide), (1, 0))


def read_tables(refs):
    return [(refs[2 * k][...], refs[2 * k + 1][...]) for k in range(4)]


def grad_kernel(factor, subs, hidden_t, error, momentum, *refs):
    residue, band_t = refs[8:]
    tables = read_tables(refs)
    kept_t = TILE // SPAN * BAND
    for k in range(subs):
        at = slice(k * TILE, (k + 1) * TILE)
        grad = jnp.dot(hidden_t[...], error[:, at], preferred_element_type=F32)
        moved = 0.999 * momentum[0, :, at] + factor * grad
        squeezed = dot3(tables[0], halves(moved), (1, 0))
        band = dot3(halves(squeezed), tables[2], (1, 0))
        band_t[k * kept_t : (k + 1) * kept_t, :] = band.T
        residue[0, :, at] = moved - decode_tile(band, tables)


def whole(a):
    return pl.BlockSpec(a.shape, lambda i: (0,) * a.ndim)


def grad_step(hidden_t, error, momentum, tables, factor):
    units, rows = hidden_t.shape
    width = error.shape[1]
    subs = 3 if width // TILE % 3 == 0 else 1
    step = TILE * subs
    tiles = width // step
    kept = units // SPAN * BAND
    kept_t = step // SPAN * BAND
    return pl.pallas_call(
        functools.partial(grad_kernel, factor, subs),
        grid=(tiles,),
        in_specs=[
            whole(hidden_t),
            pl.BlockSpec((rows, step), lambda i: (0, i)),
            pl.BlockSpec((1, units, step), lambda i: (0, 0, i)),
        ]
        + [whole(t) for t in tables],
        out_specs=[
            pl.BlockSpec((1, units, step), lambda i: (0, 0, i)),
            pl.BlockSpec((kept_t, kept), lambda i: (i, 0)),
        ],
        out_shape=[
            jax.ShapeDtypeStruct((1, units, width), F32),
            jax.ShapeDtypeStruct((tiles * kept_t, kept), F32),
        ],
        name="grad_step",
    )(hidden_t, error, momentum, *tables)


def update_kernel(replicas, subs, bands, *refs):
    update = refs[8]
    tables = read_tables(refs)
    kept_t = TILE // SPAN * BAND
    for k in range(subs):
        band = bands[k * kept_t : (k + 1) * kept_t, :].T
        tile = decode_tile(band, tables) * (1.0 / replicas)
        update[:, k * TILE : (k + 1) * TILE] = tile.astype(BF)


def update_step(bands, tables, units, width, replicas):
    rows_t, kept = bands.shape
    subs = 3 if width // TILE % 3 == 0 else 1
    step = TILE * subs
    tiles = width // step
    return pl.pallas_call(
        functools.partial(update_kernel, replicas, subs),
        grid=(tiles,),
        in_specs=[pl.BlockSpec((rows_t // tiles, kept), lambda i: (i, 0))]
        + [whole(t) for t in tables],
        out_specs=pl.BlockSpec((units, step), lambda i: (0, i)),
        out_shape=jax.ShapeDtypeStruct((units, width), BF),
        name="update_step",
    )(bands, *tables)


def make_tables(units):
    left = block_table(units // SPAN)
    right = block_table(TILE // SPAN)
    pieces = []
    for table in (left, left.T, right.T, right):
        high = table.astype(BF)
        pieces += [high, (table - high.astype(np.float32)).astype(BF)]
    return [jnp.asarray(np.ascontiguousarray(p)) for p in pieces]


def remote(src, dst, send, recv, index, axis, peer):
    return pltpu.make_async_remote_copy(
        src_ref=src,
        dst_ref=dst,
        send_sem=send.at[index],
        recv_sem=recv.at[index],
        device_id={axis: peer},
        device_id_type=pl.DeviceIdType.MESH,
    )


def greet(axis, peers):
    barrier = pltpu.get_barrier_semaphore()
    for peer in peers:
        pl.semaphore_signal(
            barrier, inc=1, device_id={axis: peer}, device_id_type=pl.DeviceIdType.MESH
        )
    pl.semaphore_wait(barrier, len(peers))


def square_kernel(
    tokens, target, weight, gate_hbm, up_hbm, down_hbm, hidden_out, error_out,
    gate, up, down, held, part, errors, from_x, from_y, relay_x, relay_y, hidden_t, hidden,
    send, recv, local,
):
    me = lax.axis_index("narrow")
    x_peer = me + 1 - 2 * (me % 2)
    y_peer = (me + 2) % 4
    rows, width = tokens.shape
    units = down.shape[0]
    half = rows // 2
    top, low = pl.ds(0, half), pl.ds(half, half)

    loads = [
        pltpu.make_async_copy(s, t, local.at[i])
        for i, (s, t) in enumerate(((gate_hbm, gate), (up_hbm, up), (down_hbm, down)))
    ]
    for load in loads:
        load.start()
    greet("narrow", (x_peer, y_peer))

    def spread(own, slots, base):
        copies = [
            remote(own.at[top], slots.at[0, top], send, recv, base, "narrow", x_peer),
            remote(own.at[low], slots.at[1, low], send, recv, base + 1, "narrow", y_peer),
            remote(own.at[low], slots.at[0, low], send, recv, base + 2, "narrow", x_peer),
            remote(own.at[top], slots.at[1, top], send, recv, base + 3, "narrow", y_peer),
            remote(slots.at[0, top], slots.at[2, top], send, recv, base + 4, "narrow", y_peer),
            remote(slots.at[1, low], slots.at[2, low], send, recv, base + 5, "narrow", x_peer),
        ]
        for copy in copies[:4]:
            copy.start()
        return copies

    def pass_on(copies):
        copies[0].wait_recv()
        copies[4].start()
        copies[1].wait_recv()
        copies[5].start()

    def expert(source, slot):
        @pl.loop(0, units // TILE)
        def _(c):
            at = pl.ds(pl.multiple_of(c * TILE, TILE), TILE)
            block = source[...]
            gated = jnp.dot(block, gate[:, at], preferred_element_type=F32)
            raised = jnp.dot(block, up[:, at], preferred_element_type=F32)
            value = gated / (1.0 + jnp.exp(-gated)) * raised
            hidden[:, at] = value.astype(BF)
            hidden_t[at, slot * rows : (slot + 1) * rows] = value.T.astype(BF)

        @pl.loop(0, width // TILE)
        def _(c):
            at = pl.ds(pl.multiple_of(c * TILE, TILE), TILE)
            part[slot, :, at] = jnp.dot(
                hidden[...], down[:, at], preferred_element_type=F32
            ).astype(BF)

    gathers = spread(tokens, held, 0)
    for load in loads:
        load.wait()
    expert(tokens, 0)
    pass_on(gathers)
    gathers[2].wait_recv()
    expert(held.at[0], 1)
    sums = [
        remote(part.at[3, top], relay_y, send, recv, 6, "narrow", x_peer),
        remote(part.at[3, low], relay_x, send, recv, 7, "narrow", y_peer),
        remote(part.at[1, top], from_x.at[top], send, recv, 8, "narrow", x_peer),
        remote(part.at[2, low], from_y.at[low], send, recv, 9, "narrow", y_peer),
        remote(part.at[1, low], from_x.at[low], send, recv, 10, "narrow", x_peer),
        remote(part.at[2, top], from_y.at[top], send, recv, 11, "narrow", y_peer),
    ]
    sums[2].start()
    gathers[3].wait_recv()
    expert(held.at[1], 2)
    sums[3].start()
    gathers[4].wait_recv()
    gathers[5].wait_recv()
    expert(held.at[2], 3)
    sums[0].start()
    sums[1].start()
    hidden_store = pltpu.make_async_copy(hidden_t, hidden_out, local.at[3])
    hidden_store.start()

    step = 16

    def add_rows(slot, first, arrived):
        @pl.loop(0, half // step)
        def _(c):
            mine = pl.ds(pl.multiple_of(first + c * step, step), step)
            theirs = pl.ds(pl.multiple_of(c * step, step), step)
            part[slot, mine, :] = (
                part[slot, mine, :].astype(F32) + arrived[theirs, :].astype(F32)
            ).astype(BF)

    def error_rows(first):
        @pl.loop(0, half // step)
        def _(c):
            at = pl.ds(pl.multiple_of(first + c * step, step), step)
            total = (
                part[0, at, :].astype(F32)
                + from_x[at, :].astype(F32)
                + from_y[at, :].astype(F32)
            )
            scale = weight[at, :]
            value = scale * (scale * total - target[at, :].astype(F32))
            errors[0, at, :] = value.astype(BF)

    sums[0].wait_recv()
    add_rows(2, 0, relay_y)
    sums[5].start()
    sums[1].wait_recv()
    add_rows(1, half, relay_x)
    sums[4].start()
    sums[2].wait_recv()
    sums[5].wait_recv()
    error_rows(0)
    sums[3].wait_recv()
    sums[4].wait_recv()
    error_rows(half)
    shared = spread(errors.at[0], errors.at[pl.ds(1, 3)], 12)
    stores = [
        pltpu.make_async_copy(errors.at[i], error_out.at[i], local.at[4 + i]) for i in range(4)
    ]
    stores[0].start()
    pass_on(shared)
    shared[2].wait_recv()
    stores[1].start()
    shared[3].wait_recv()
    stores[2].start()
    shared[4].wait_recv()
    shared[5].wait_recv()
    stores[3].start()
    for copy in gathers + sums + shared:
        copy.wait_send()
    hidden_store.wait()
    for store in stores:
        store.wait()


def square_forward(tokens, target, combine, filled, w_gate, w_up, w_down):
    rows, width = tokens.shape
    units = w_down.shape[0]
    half = rows // 2
    row_ids = lax.axis_index("narrow") * rows + jnp.arange(rows, dtype=jnp.int32)
    weight = jnp.where(row_ids < filled[0], combine.astype(F32), 0.0)[:, None]
    vmem = pl.BlockSpec(memory_space=pltpu.VMEM)
    hbm = pl.BlockSpec(memory_space=pl.ANY)
    block = lambda *shape: pltpu.VMEM(shape, BF)
    hidden_t, errors = pl.pallas_call(
        square_kernel,
        in_specs=[vmem] * 3 + [hbm] * 3,
        out_specs=[hbm] * 2,
        out_shape=[
            jax.ShapeDtypeStruct((units, 4 * rows), BF),
            jax.ShapeDtypeStruct((4, rows, width), BF),
        ],
        scratch_shapes=[
            block(width, units), block(width, units), block(units, width),
            block(3, rows, width), block(4, rows, width), block(4, rows, width),
            block(rows, width), block(rows, width), block(half, width), block(half, width),
            block(units, 4 * rows), block(rows, units),
            pltpu.SemaphoreType.DMA((18,)), pltpu.SemaphoreType.DMA((18,)),
            pltpu.SemaphoreType.DMA((8,)),
        ],
        compiler_params=pltpu.CompilerParams(
            collective_id=0, has_side_effects=True, vmem_limit_bytes=60 << 20
        ),
        name="square_forward",
    )(tokens, target, weight, w_gate, w_up, w_down)
    return hidden_t, errors.reshape(4 * rows, width)


def band_kernel(count, band, total, outgoing, arrived, summed, gathered, send, recv):
    me = lax.axis_index("wide")
    peers = [(me + k) % count for k in range(1, count)]
    greet("wide", peers)
    share = band.shape[0] // count
    outgoing[...] = band[...].reshape(count, share, band.shape[1]).astype(BF)
    first = [
        remote(outgoing.at[p], arrived.at[k], send, recv, k, "wide", p)
        for k, p in enumerate(peers)
    ]
    for copy in first:
        copy.start()
    amount = outgoing[me].astype(F32)
    for k, copy in enumerate(first):
        copy.wait_recv()
        amount = amount + arrived[k].astype(F32)
    summed[...] = amount.astype(BF)
    second = [
        remote(summed, gathered.at[me], send, recv, count + k, "wide", p)
        for k, p in enumerate(peers)
    ]
    for copy in second:
        copy.start()
    for copy in second:
        copy.wait_recv()
    for copy in first + second:
        copy.wait_send()
    gathered[me] = summed[...]
    total[...] = gathered[...].astype(F32).reshape(band.shape)


def band_sum(band, count):
    share = band.shape[0] // count
    vmem = pl.BlockSpec(memory_space=pltpu.VMEM)
    block = lambda *shape: pltpu.VMEM(shape + (share, band.shape[1]), BF)
    return pl.pallas_call(
        functools.partial(band_kernel, count),
        in_specs=[vmem],
        out_specs=vmem,
        out_shape=jax.ShapeDtypeStruct(band.shape, F32),
        scratch_shapes=[
            block(count), block(count - 1), block(), block(count),
            pltpu.SemaphoreType.DMA((2 * count,)), pltpu.SemaphoreType.DMA((2 * count,)),
        ],
        compiler_params=pltpu.CompilerParams(collective_id=1, has_side_effects=True),
        name="band_sum",
    )(band)


def forward(tokens, target, combine, filled, w_gate, w_up, w_down):
    local_rows = tokens.shape[0]
    piece = lax.all_gather(tokens, "narrow", axis=0, tiled=True)
    gate_proj = jnp.dot(piece, w_gate, preferred_element_type=F32)
    up_proj = jnp.dot(piece, w_up, preferred_element_type=F32)
    hidden = (jax.nn.silu(gate_proj) * up_proj).astype(BF)
    summed = lax.psum_scatter(
        jnp.dot(hidden, w_down, preferred_element_type=F32).astype(BF),
        "narrow",
        scatter_dimension=0,
        tiled=True,
    ).astype(F32)
    weight = combine.astype(F32)[:, None]
    row_ids = lax.axis_index("narrow") * local_rows + jnp.arange(local_rows, dtype=jnp.int32)
    error = jnp.where(
        (row_ids < filled[0])[:, None], weight * (weight * summed - target.astype(F32)), 0.0
    ).astype(BF)
    return hidden.T, lax.all_gather(error, "narrow", axis=0, tiled=True)


def body(tokens, target, combine, filled, w_gate, w_up, w_down, momentum):
    units, width = w_down.shape
    narrow, replicas = lax.axis_size("narrow"), lax.axis_size("wide")
    total_rows = tokens.shape[0] * narrow
    tables = make_tables(units)
    step = square_forward if narrow == 4 else forward
    hidden_t, errors = step(tokens, target, combine, filled, w_gate, w_up, w_down)
    residue, band = grad_step(hidden_t, errors, momentum, tables, 1.0 / math.sqrt(total_rows))
    if narrow == 4:
        total = band_sum(band, replicas)
    else:
        bands = lax.all_gather(band.astype(BF)[None], "wide", axis=0, tiled=True)
        total = jnp.sum(bands.astype(F32), axis=0)
    return residue, update_step(total, tables, units, width, replicas)


def solution(mesh):
    in_specs = (
        P(("wide", "narrow"), None),
        P(("wide", "narrow"), None),
        P(("wide", "narrow")),
        P("wide"),
        P(None, "narrow"),
        P(None, "narrow"),
        P("narrow", None),
        P("wide", "narrow", None),
    )
    out_specs = (P("wide", "narrow", None), P("narrow", None))
    return jax.shard_map(body, mesh=mesh, in_specs=in_specs, out_specs=out_specs, check_vma=False)
```

profile of v0, /device:TPU:0, one launch (start us, length us, event | category | flops | bytes accessed | tf_op | source)
XLA Modules:
  0.0 163.5 jit_solution(9801262823238834164)
XLA Ops:
  1.3 0.7 compare_select_fusion
  1.9 0.8 copy.18.weight
  2.7 124.5 %square_forward.1 = (bf16[512,1024]{1,0:T(8,128)(2,1)}, bf16[4,256,2304]{2,1,0:T(8,128)(2,1)}) custom-call(bf16[256,2304]{1,0:T(8,128)(2,1)} %tokens.1, bf16[256,2304]{1,0:T(8,128)(2,1)} %target.1, f32[256,1]{1,0:T(8,128)} %copy.18.weight, bf16[2304,512]{1,0:T(8,128)(2,1)} %gate_hbm.1, bf16[2304,512]{1,0:T(8,128)(2,1)} %up_hbm.1, bf16[512,2304]{1,0:T(8,128)(2,1)} %down_hbm.1), custom_call_target="tpu_custom_call" | custom-call | tf_op jit(solution)/shard_map/square_forward/pallas_call | solution.py:300
  127.2 15.6 %grad_step.1 = (f32[1,512,2304]{2,1,0:T(8,128)}, f32[576,128]{1,0:T(8,128)}) custom-call(bf16[512,1024]{1,0:T(8,128)(2,1)} %get-tuple-element.6.hidden_t, bf16[1024,2304]{1,0:T(8,128)(2,1)} %bitcast.4, f32[1,512,2304]{2,1,0:T(8,128)} %momentum.1, bf16[128,512]{1,0:T(8,128)(2,1)} %constant.24.clone.refs_0_, bf16[128,512]{1,0:T(8,128)(2,1)} %constant.25.clone.refs_1_, ...), custom_call_target="tpu_custom_call" | custom-call | tf_op jit(solution)/shard_map/grad_step/pallas_call | solution.py:73
  142.8 14.6 %band_sum.1.bands = f32[576,128]{1,0:T(8,128)} custom-call(f32[576,128]{1,0:T(8,128)} %get-tuple-element.9.band), custom_call_target="tpu_custom_call" | custom-call | tf_op jit(solution)/shard_map/band_sum/pallas_call | solution.py:359
  157.5 6.1 %update_step.1 = bf16[512,2304]{1,0:T(8,128)(2,1)} custom-call(f32[576,128]{1,0:T(8,128)} %band_sum.1.bands, bf16[128,512]{1,0:T(8,128)(2,1)} %constant.24.clone.refs_0_, bf16[128,512]{1,0:T(8,128)(2,1)} %constant.25.clone.refs_1_, bf16[512,128]{1,0:T(8,128)(2,1)} %constant.26.clone.refs_2_, bf16[512,128]{1,0:T(8,128)(2,1)} %constant.27.clone.refs_3_, ...), custom_call_target="tpu_custom_call" | custom-call | tf_op jit(solution)/shard_map/update_step/pallas_call | solution.py:109
where the time goes:
time: 164 us
  Pallas kernels  161 us (98%)
    pallas_call x1, Pallas kernels, square_forward(): pl.pallas_call(square_kernel, in_specs=[vmem] * 3 + [hbm] * 3, out_specs=...  124 us
    pallas_call x1, Pallas kernels, grad_step(): pl.pallas_call(functools.partial(grad_kernel, factor, subs), grid=(tiles,...  15.6 us
    pallas_call x1, Pallas kernels, band_sum(): pl.pallas_call(functools.partial(band_kernel, count), in_specs=[vmem], ou...  14.6 us
    pallas_call x1, Pallas kernels, update_step(): pl.pallas_call(functools.partial(update_kernel, replicas, subs), grid=(ti...  6.07 us

commit v1 on v0

--- a/solution.py
+++ b/solution.py
@@ -147,178 +147,346 @@
     pl.semaphore_wait(barrier, len(peers))
 
 
-def square_kernel(
-    tokens, target, weight, gate_hbm, up_hbm, down_hbm, hidden_out, error_out,
-    gate, up, down, held, part, errors, from_x, from_y, relay_x, relay_y, hidden_t, hidden,
-    send, recv, local,
+def split_kernel(
+    factor, tokens_hbm, target_hbm, combine, filled, gate_hbm, up_hbm, down_hbm, momentum_hbm, *refs
 ):
-    me = lax.axis_index("narrow")
+    tables_hbm, (residue_hbm, band_t) = refs[:8], refs[8:10]
+    (
+        tok, target, weight, gate, up, gate_y, up_y, down, hidden, hidden_t, lent_t,
+        kept, sent, came, errors, state,
+    ) = refs[10:26]
+    tables_vmem = refs[26:34]
+    send, recv, local = refs[34:37]
+    me, place = lax.axis_index("narrow"), lax.axis_index("wide")
     x_peer = me + 1 - 2 * (me % 2)
     y_peer = (me + 2) % 4
-    rows, width = tokens.shape
-    units = down.shape[0]
-    half = rows // 2
-    top, low = pl.ds(0, half), pl.ds(half, half)
-
+    twin = place + 1 - 2 * (place % 2)
+    z_peer = place + 2 - 4 * (place // 2 % 2)
+    quarter = place % 4
+    rows, width = target.shape
+    units = gate.shape[1]
+    deep, flat = width // 4, units // 4
+    half = deep // 2
+    chunks = width // TILE
+    parts = 4 * (units // TILE)
+
+    sizes = [2] + [parts] * 4 + [chunks] * 4 + [units // TILE] + [chunks] * 4
+    starts = [sum(sizes[:k]) for k in range(len(sizes) + 1)]
+
+    def link(kind, index, src, dst, axis, peer):
+        return remote(src, dst, send, recv, starts[kind] + index, axis, peer)
+
+    def cols(c):
+        if isinstance(c, int):
+            return pl.ds(c * TILE, TILE)
+        return pl.ds(pl.multiple_of(c * TILE, TILE), TILE)
+
+    def token_copy(k):
+        part = rows // 2
+        src = tokens_hbm.at[pl.ds(k * part, part)]
+        return link(0, k, src, tok.at[pl.ds(rows + k * part, part)], "narrow", x_peer)
+
+    def piece(k, ref, owner):
+        first = pl.multiple_of(owner * deep + k % 2 * half, 32)
+        return ref.at[pl.ds(first, half), cols(k // 4)]
+
+    def weight_copy(kind, k):
+        mine, theirs = ((gate_hbm, gate_y), (up_hbm, up_y))[k // 2 % 2]
+        if kind == 1:
+            return link(1, k, piece(k, mine, quarter), piece(k, theirs, quarter), "narrow", y_peer)
+        if kind == 4:
+            there = piece(k, theirs, (quarter + 2) % 4)
+            return link(4, k, there, there, "wide", twin)
+        here = piece(k, theirs, quarter)
+        return link(kind, k, here, here, "wide", z_peer if kind == 2 else twin)
+
+    def down_piece(c, ref, first, owner):
+        return ref.at[pl.ds(pl.multiple_of(first + owner * flat, 32), flat), cols(c)]
+
+    def down_copy(kind, c):
+        if kind == 5:
+            src = down_piece(c, down_hbm, 0, quarter)
+            return link(5, c, src, down_piece(c, down, units, quarter), "narrow", y_peer)
+        if kind == 8:
+            there = down_piece(c, down, units, (quarter + 2) % 4)
+            return link(8, c, there, there, "wide", twin)
+        here = down_piece(c, down, units, quarter)
+        return link(kind, c, here, here, "wide", z_peer if kind == 6 else twin)
+
+    def lend_copy(t):
+        at = pl.ds(t * TILE, TILE)
+        dst = hidden_t.at[at, pl.ds(2 * rows, 2 * rows)]
+        return link(9, t, lent_t.at[at], dst, "narrow", y_peer)
+
+    def sum_copy(c):
+        return link(10, c, sent.at[:, cols(c)], came.at[:, cols(c)], "narrow", x_peer)
+
+    def slot(k, c):
+        return errors.at[pl.ds(k * rows, rows), cols(c)]
+
+    def error_x(c):
+        return link(11, c, slot(0, c), slot(1, c), "narrow", x_peer)
+
+    def error_y(c):
+        return link(12, c, slot(0, c), slot(2, c), "narrow", y_peer)
+
+    def relay_by_y(c):
+        return link(13, c, slot(1, c), slot(3, c), "narrow", y_peer)
+
+    def relay_by_x(c):
+        return link(13, c, slot(2, c), slot(3, c), "narrow", x_peer)
+
+    def load(k, src, dst):
+        return pltpu.make_async_copy(src, dst, local.at[k])
+
+    barrier = pltpu.get_barrier_semaphore()
+    for axis, peer in (("narrow", x_peer), ("narrow", y_peer), ("wide", twin), ("wide", z_peer)):
+        pl.semaphore_signal(
+            barrier, inc=1, device_id={axis: peer}, device_id_type=pl.DeviceIdType.MESH
+        )
     loads = [
-        pltpu.make_async_copy(s, t, local.at[i])
-        for i, (s, t) in enumerate(((gate_hbm, gate), (up_hbm, up), (down_hbm, down)))
+        load(0, tokens_hbm, tok.at[pl.ds(0, rows)]),
+        load(1, gate_hbm, gate),
+        load(2, up_hbm, up),
+        load(3, down_hbm, down.at[pl.ds(0, units)]),
+        load(4, target_hbm, target),
+        load(5, momentum_hbm.at[0], state),
     ]
-    for load in loads:
-        load.start()
-    greet("narrow", (x_peer, y_peer))
-
-    def spread(own, slots, base):
-        copies = [
-            remote(own.at[top], slots.at[0, top], send, recv, base, "narrow", x_peer),
-            remote(own.at[low], slots.at[1, low], send, recv, base + 1, "narrow", y_peer),
-            remote(own.at[low], slots.at[0, low], send, recv, base + 2, "narrow", x_peer),
-            remote(own.at[top], slots.at[1, top], send, recv, base + 3, "narrow", y_peer),
-            remote(slots.at[0, top], slots.at[2, top], send, recv, base + 4, "narrow", y_peer),
-            remote(slots.at[1, low], slots.at[2, low], send, recv, base + 5, "narrow", x_peer),
-        ]
-        for copy in copies[:4]:
-            copy.start()
-        return copies
-
-    def pass_on(copies):
-        copies[0].wait_recv()
-        copies[4].start()
-        copies[1].wait_recv()
-        copies[5].start()
-
-    def expert(source, slot):
-        @pl.loop(0, units // TILE)
-        def _(c):
-            at = pl.ds(pl.multiple_of(c * TILE, TILE), TILE)
-            block = source[...]
-            gated = jnp.dot(block, gate[:, at], preferred_element_type=F32)
-            raised = jnp.dot(block, up[:, at], preferred_element_type=F32)
-            value = gated / (1.0 + jnp.exp(-gated)) * raised
-            hidden[:, at] = value.astype(BF)
-            hidden_t[at, slot * rows : (slot + 1) * rows] = value.T.astype(BF)
-
-        @pl.loop(0, width // TILE)
-        def _(c):
-            at = pl.ds(pl.multiple_of(c * TILE, TILE), TILE)
-            part[slot, :, at] = jnp.dot(
-                hidden[...], down[:, at], preferred_element_type=F32
-            ).astype(BF)
-
-    gathers = spread(tokens, held, 0)
-    for load in loads:
-        load.wait()
-    expert(tokens, 0)
-    pass_on(gathers)
-    gathers[2].wait_recv()
-    expert(held.at[0], 1)
-    sums = [
-        remote(part.at[3, top], relay_y, send, recv, 6, "narrow", x_peer),
-        remote(part.at[3, low], relay_x, send, recv, 7, "narrow", y_peer),
-        remote(part.at[1, top], from_x.at[top], send, recv, 8, "narrow", x_peer),
-        remote(part.at[2, low], from_y.at[low], send, recv, 9, "narrow", y_peer),
-        remote(part.at[1, low], from_x.at[low], send, recv, 10, "narrow", x_peer),
-        remote(part.at[2, top], from_y.at[top], send, recv, 11, "narrow", y_peer),
-    ]
-    sums[2].start()
-    gathers[3].wait_recv()
-    expert(held.at[1], 2)
-    sums[3].start()
-    gathers[4].wait_recv()
-    gathers[5].wait_recv()
-    expert(held.at[2], 3)
-    sums[0].start()
-    sums[1].start()
-    hidden_store = pltpu.make_async_copy(hidden_t, hidden_out, local.at[3])
-    hidden_store.start()
-
-    step = 16
-
-    def add_rows(slot, first, arrived):
-        @pl.loop(0, half // step)
-        def _(c):
-            mine = pl.ds(pl.multiple_of(first + c * step, step), step)
-            theirs = pl.ds(pl.multiple_of(c * step, step), step)
-            part[slot, mine, :] = (
-                part[slot, mine, :].astype(F32) + arrived[theirs, :].astype(F32)
-            ).astype(BF)
-
-    def error_rows(first):
-        @pl.loop(0, half // step)
-        def _(c):
-            at = pl.ds(pl.multiple_of(first + c * step, step), step)
-            total = (
-                part[0, at, :].astype(F32)
-                + from_x[at, :].astype(F32)
-                + from_y[at, :].astype(F32)
-            )
-            scale = weight[at, :]
-            value = scale * (scale * total - target[at, :].astype(F32))
-            errors[0, at, :] = value.astype(BF)
-
-    sums[0].wait_recv()
-    add_rows(2, 0, relay_y)
-    sums[5].start()
-    sums[1].wait_recv()
-    add_rows(1, half, relay_x)
-    sums[4].start()
-    sums[2].wait_recv()
-    sums[5].wait_recv()
-    error_rows(0)
-    sums[3].wait_recv()
-    sums[4].wait_recv()
-    error_rows(half)
-    shared = spread(errors.at[0], errors.at[pl.ds(1, 3)], 12)
-    stores = [
-        pltpu.make_async_copy(errors.at[i], error_out.at[i], local.at[4 + i]) for i in range(4)
-    ]
-    stores[0].start()
-    pass_on(shared)
-    shared[2].wait_recv()
-    stores[1].start()
-    shared[3].wait_recv()
-    stores[2].start()
-    shared[4].wait_recv()
-    shared[5].wait_recv()
-    stores[3].start()
-    for copy in gathers + sums + shared:
-        copy.wait_send()
-    hidden_store.wait()
-    for store in stores:
-        store.wait()
-
-
-def square_forward(tokens, target, combine, filled, w_gate, w_up, w_down):
+    loads += [load(6 + k, s, d) for k, (s, d) in enumerate(zip(tables_hbm, tables_vmem))]
+    for copy in loads:
+        copy.start()
+    pl.semaphore_wait(barrier, 4)
+    for k in range(2):
+        token_copy(k).start()
+    for k in range(parts):
+        weight_copy(1, k).start()
+
+    @pl.loop(0, chunks)
+    def _(c):
+        down_copy(5, c).start()
+
+    row_ids = me * rows + lax.broadcasted_iota(jnp.int32, combine.shape, 1)
+    live = jnp.where(row_ids < filled[0], combine[...].astype(F32), 0.0)
+    weight[...] = jnp.broadcast_to(live, (weight.shape[1], rows)).T
+
+    def expert(first, count, gates, ups, base, turned, t):
+        block = tok[first : first + count, :]
+        gated = jnp.dot(block, gates[:, cols(t)], preferred_element_type=F32)
+        raised = jnp.dot(block, ups[:, cols(t)], preferred_element_type=F32)
+        value = gated / (1.0 + jnp.exp(-gated)) * raised
+        hidden[first : first + count, base + t * TILE : base + (t + 1) * TILE] = value.astype(BF)
+        turned[t * TILE : (t + 1) * TILE, first : first + count] = value.T.astype(BF)
+
+    def pass_weight(k):
+        weight_copy(1, k).wait_recv()
+        weight_copy(2, k).start()
+        weight_copy(3, k).start()
+
+    def share_weight(k):
+        weight_copy(2, k).wait_recv()
+        weight_copy(4, k).start()
+
+    def take_weights(first, count):
+        for k in range(first, first + count):
+            weight_copy(3, k).wait_recv()
+            weight_copy(4, k).wait_recv()
+
+    def pass_down(c):
+        down_copy(5, c).wait_recv()
+        down_copy(6, c).start()
+        down_copy(7, c).start()
+
+    def share_down(c):
+        down_copy(6, c).wait_recv()
+        down_copy(8, c).start()
+
+    def take_down(c):
+        down_copy(7, c).wait_recv()
+        down_copy(8, c).wait_recv()
+
+    def partial(c):
+        part = jnp.dot(hidden[...], down[:, cols(c)], preferred_element_type=F32)
+        kept[:, cols(c)] = part[:rows]
+        sent[:, cols(c)] = part[rows:].astype(BF)
+        sum_copy(c).start()
+
+    def error(c):
+        sum_copy(c).wait_recv()
+        total = kept[:, cols(c)] + came[:, cols(c)].astype(F32)
+        scale = jnp.concatenate([weight[...]] * (TILE // weight.shape[1]), axis=1)
+        value = scale * (scale * total - target[:, cols(c)].astype(F32))
+        errors[pl.ds(0, rows), cols(c)] = value.astype(BF)
+        error_x(c).start()
+        error_y(c).start()
+
+    def relay(c):
+        @pl.when(c % 3 != 2)
+        def _():
+            error_x(c).wait_recv()
+            relay_by_y(c).start()
+
+        @pl.when(c % 3 == 2)
+        def _():
+            error_y(c).wait_recv()
+            relay_by_x(c).start()
+
+    tables = lambda: [(tables_vmem[2 * k][...], tables_vmem[2 * k + 1][...]) for k in range(4)]
+
+    def store(c):
+        return pltpu.make_async_copy(
+            state.at[:, cols(c)], residue_hbm.at[0, :, cols(c)], local.at[14 + c]
+        )
+
+    kept_t = TILE // SPAN * BAND
+
+    def gradient(c):
+        @pl.when(c % 3 != 2)
+        def _():
+            error_y(c).wait_recv()
+
+        @pl.when(c % 3 == 2)
+        def _():
+            error_x(c).wait_recv()
+
+        relay_by_y(c).wait_recv()
+        grad = jnp.dot(hidden_t[...], errors[:, cols(c)], preferred_element_type=F32)
+        moved = 0.999 * state[:, cols(c)] + factor * grad
+        table = tables()
+        squeezed = dot3(table[0], halves(moved), (1, 0))
+        band = dot3(halves(squeezed), table[2], (1, 0))
+        band_t[pl.ds(pl.multiple_of(c * kept_t, kept_t), kept_t), :] = band.T
+        state[:, cols(c)] = moved - decode_tile(band, table)
+        store(c).start()
+
+    for k in range(3):
+        loads[k].wait()
+    for t in range(units // TILE):
+        expert(0, rows, gate, up, 0, hidden_t, t)
+    pass_weight(0)
+    for k in range(1, 6):
+        pass_weight(k)
+        if k < 5:
+            share_weight(k - 1)
+    take_weights(0, 4)
+    expert(0, rows, gate_y, up_y, units, lent_t, 0)
+    share_weight(4)
+    pass_weight(6)
+    share_weight(5)
+    pass_weight(7)
+    for k in range(2):
+        token_copy(k).wait_recv()
+    for t in range(units // TILE):
+        expert(rows, rows, gate, up, 0, hidden_t, t)
+    share_weight(6)
+    expert(rows, rows, gate_y, up_y, units, lent_t, 0)
+    lend_copy(0).start()
+    share_weight(7)
+    for c in range(3):
+        pass_down(c)
+    share_down(0)
+    take_weights(4, 4)
+    expert(0, 2 * rows, gate_y, up_y, units, lent_t, 1)
+    lend_copy(1).start()
+    for copy in loads[3:]:
+        copy.wait()
+    share_down(1)
+    take_down(0)
+    pass_down(3)
+    partial(0)
+    share_down(2)
+    take_down(1)
+    pass_down(4)
+    partial(1)
+
+    lag = 3
+
+    @pl.loop(0, chunks + lag)
+    def _(c):
+        @pl.when(c < chunks)
+        def _():
+            error(c)
+
+        @pl.when((c >= 1) & (c <= chunks))
+        def _():
+            relay(c - 1)
+
+        @pl.when(c + 5 < chunks)
+        def _():
+            pass_down(c + 5)
+
+        @pl.when(c + 3 < chunks)
+        def _():
+            share_down(c + 3)
+
+        @pl.when(c + 2 < chunks)
+        def _():
+            take_down(c + 2)
+            partial(c + 2)
+
+        @pl.when(c == 0)
+        def _():
+            for t in range(units // TILE):
+                lend_copy(t).wait_recv()
+
+        @pl.when(c >= lag)
+        def _():
+            gradient(c - lag)
+
+    for k in range(2):
+        token_copy(k).wait_send()
+    for k in range(parts):
+        for kind in range(1, 5):
+            weight_copy(kind, k).wait_send()
+    for t in range(units // TILE):
+        lend_copy(t).wait_send()
+
+    @pl.loop(0, chunks)
+    def _(c):
+        for kind in range(5, 9):
+            down_copy(kind, c).wait_send()
+        sum_copy(c).wait_send()
+        error_x(c).wait_send()
+        error_y(c).wait_send()
+        relay_by_y(c).wait_send()
+        store(c).wait()
+
+
+def split_step(tokens, target, combine, filled, w_gate, w_up, w_down, momentum, tables, factor):
     rows, width = tokens.shape
     units = w_down.shape[0]
-    half = rows // 2
-    row_ids = lax.axis_index("narrow") * rows + jnp.arange(rows, dtype=jnp.int32)
-    weight = jnp.where(row_ids < filled[0], combine.astype(F32), 0.0)[:, None]
     vmem = pl.BlockSpec(memory_space=pltpu.VMEM)
     hbm = pl.BlockSpec(memory_space=pl.ANY)
     block = lambda *shape: pltpu.VMEM(shape, BF)
-    hidden_t, errors = pl.pallas_call(
-        square_kernel,
-        in_specs=[vmem] * 3 + [hbm] * 3,
-        out_specs=[hbm] * 2,
+    chunks = width // TILE
+    tiles = units // TILE
+    count = 2 + 16 * tiles + 8 * chunks + tiles
+    return pl.pallas_call(
+        functools.partial(split_kernel, factor),
+        in_specs=[hbm, hbm, vmem, pl.BlockSpec(memory_space=pltpu.SMEM)] + [hbm] * 12,
+        out_specs=[hbm, vmem],
         out_shape=[
-            jax.ShapeDtypeStruct((units, 4 * rows), BF),
-            jax.ShapeDtypeStruct((4, rows, width), BF),
+            jax.ShapeDtypeStruct((1, units, width), F32),
+            jax.ShapeDtypeStruct((width // SPAN * BAND, units // SPAN * BAND), F32),
         ],
         scratch_shapes=[
-            block(width, units), block(width, units), block(units, width),
-            block(3, rows, width), block(4, rows, width), block(4, rows, width),
-            block(rows, width), block(rows, width), block(half, width), block(half, width),
-            block(units, 4 * rows), block(rows, units),
-            pltpu.SemaphoreType.DMA((18,)), pltpu.SemaphoreType.DMA((18,)),
-            pltpu.SemaphoreType.DMA((8,)),
+            block(2 * rows, width), block(rows, width), pltpu.VMEM((rows, 128), F32),
+            block(width, units), block(width, units), block(width, units), block(width, units),
+            block(2 * units, width), block(2 * rows, 2 * units), block(units, 4 * rows),
+            block(units, 2 * rows), pltpu.VMEM((rows, width), F32), block(rows, width),
+            block(rows, width), block(4 * rows, width), pltpu.VMEM((units, width), F32),
+        ]
+        + [block(*t.shape) for t in tables]
+        + [
+            pltpu.SemaphoreType.DMA((count,)), pltpu.SemaphoreType.DMA((count,)),
+            pltpu.SemaphoreType.DMA((14 + chunks,)),
         ],
         compiler_params=pltpu.CompilerParams(
             collective_id=0, has_side_effects=True, vmem_limit_bytes=60 << 20
         ),
-        name="square_forward",
-    )(tokens, target, weight, w_gate, w_up, w_down)
-    return hidden_t, errors.reshape(4 * rows, width)
+        name="split_step",
+    )(
+        tokens, target, combine.reshape(1, rows), filled, w_gate, w_up, w_down, momentum, *tables
+    )
 
 
 def band_kernel(count, band, total, outgoing, arrived, summed, gathered, send, recv):
@@ -395,12 +563,16 @@
     narrow, replicas = lax.axis_size("narrow"), lax.axis_size("wide")
     total_rows = tokens.shape[0] * narrow
     tables = make_tables(units)
-    step = square_forward if narrow == 4 else forward
-    hidden_t, errors = step(tokens, target, combine, filled, w_gate, w_up, w_down)
-    residue, band = grad_step(hidden_t, errors, momentum, tables, 1.0 / math.sqrt(total_rows))
-    if narrow == 4:
+    factor = 1.0 / math.sqrt(total_rows)
+    fits = units == 2 * TILE and width % TILE == 0 and tokens.shape[0] % 128 == 0
+    if narrow == 4 and replicas % 4 == 0 and fits:
+        residue, band = split_step(
+            tokens, target, combine, filled, w_gate, w_up, w_down, momentum, tables, factor
+        )
         total = band_sum(band, replicas)
     else:
+        hidden_t, errors = forward(tokens, target, combine, filled, w_gate, w_up, w_down)
+        residue, band = grad_step(hidden_t, errors, momentum, tables, factor)
         bands = lax.all_gather(band.astype(BF)[None], "wide", axis=0, tiled=True)
         total = jnp.sum(bands.astype(F32), axis=0)
     return residue, update_step(total, tables, units, width, replicas)

time: 164 us -> 140 us (0.85)
  Pallas kernels: 161 us -> 132 us
  local copies, waits for them, and re-layouts: 0.8 us -> 6.05 us
    pallas_call x2 -> x1, Pallas kernels: 140 us -> 112 us  [split_step(): pl.pallas_call(functools.partial(split_kernel, factor), in_specs=[hbm, hb...]
    unnamed x0 -> x1, local copies, waits for them, and re-layouts: none -> 4.82 us
where the time goes in v1:
time: 140 us; the launch traced here: 139 us
  Pallas kernels  132 us (94%)
  local copies, waits for them, and re-layouts  6.05 us (4%)
    pallas_call x1, Pallas kernels, split_step(): pl.pallas_call(functools.partial(split_kernel, factor), in_specs=[hbm, hb...  112 us
    pallas_call x1, Pallas kernels, band_sum(): pl.pallas_call(functools.partial(band_kernel, count), in_specs=[vmem], ou...  14.2 us
    pallas_call x1, Pallas kernels, update_step(): pl.pallas_call(functools.partial(update_kernel, replicas, subs), grid=(ti...  6.07 us
    unnamed x1, local copies, waits for them, and re-layouts  4.82 us

profile of v1, /device:TPU:0, one launch (start us, length us, event | category | flops | bytes accessed | tf_op | source)
XLA Modules:
  0.0 139.5 jit_solution(10882282466416196310)
XLA Ops:
  1.3 1.2 reshape.7.combine
  2.5 111.8 %split_step.1 = (f32[1,512,2304]{2,1,0:T(8,128)}, f32[576,128]{1,0:T(8,128)}) custom-call(bf16[256,2304]{1,0:T(8,128)(2,1)} %tokens_hbm.1, bf16[256,2304]{1,0:T(8,128)(2,1)} %target_hbm.1, bf16[1,256]{1,0:T(2,128)(2,1)} %reshape.7.combine, s32[1]{0:T(128)S(6)} %copy.19.filled, bf16[2304,512]{1,0:T(8,128)(2,1)} %gate_hbm.1, bf16[2304,512]{1,0:T(8,128)(2,1)} %up_hbm.1, ...), custom_call_target="tpu_custom_call" | custom-call | tf_op jit(solution)/shard_map/split_step/pallas_call | solution.py:463
  114.3 14.2 %band_sum.1.bands = f32[576,128]{1,0:T(8,128)} custom-call(f32[576,128]{1,0:T(8,128)} %get-tuple-element.5.band), custom_call_target="tpu_custom_call" | custom-call | tf_op jit(solution)/shard_map/band_sum/pallas_call | solution.py:527
  128.6 6.1 %update_step.1 = bf16[512,2304]{1,0:T(8,128)(2,1)} custom-call(f32[576,128]{1,0:T(8,128)} %band_sum.1.bands, bf16[128,512]{1,0:T(8,128)(2,1)} %constant.16.clone.refs_0_, bf16[128,512]{1,0:T(8,128)(2,1)} %constant.17.clone.refs_1_, bf16[512,128]{1,0:T(8,128)(2,1)} %constant.18.clone.refs_2_, bf16[512,128]{1,0:T(8,128)(2,1)} %constant.19.clone.refs_3_, ...), custom_call_target="tpu_custom_call" | custom-call | tf_op jit(solution)/shard_map/update_step/pallas_call | solution.py:109
  134.6 4.8 %copy.20 = f32[1,512,2304]{2,1,0:T(8,128)} copy(f32[1,512,2304]{2,1,0:T(8,128)} %get-tuple-element.8) | data formatting | bytes 9437184

commit v2 on v1

--- a/solution.py
+++ b/solution.py
@@ -138,25 +138,16 @@
     )
 
 
-def greet(axis, peers):
-    barrier = pltpu.get_barrier_semaphore()
-    for peer in peers:
-        pl.semaphore_signal(
-            barrier, inc=1, device_id={axis: peer}, device_id_type=pl.DeviceIdType.MESH
-        )
-    pl.semaphore_wait(barrier, len(peers))
-
-
 def split_kernel(
-    factor, tokens_hbm, target_hbm, combine, filled, gate_hbm, up_hbm, down_hbm, momentum_hbm, *refs
+    factor, replicas, tokens_hbm, target_hbm, combine, filled, gate_hbm, up_hbm, down_hbm, momentum_hbm, *refs
 ):
-    tables_hbm, (residue_hbm, band_t) = refs[:8], refs[8:10]
+    tables_hbm, (residue_hbm, update_hbm) = refs[:8], refs[8:10]
     (
         tok, target, weight, gate, up, gate_y, up_y, down, hidden, hidden_t, lent_t,
-        kept, sent, came, errors, state,
-    ) = refs[10:26]
-    tables_vmem = refs[26:34]
-    send, recv, local = refs[34:37]
+        kept, sent, came, errors, state, bands, update,
+    ) = refs[10:28]
+    tables_vmem = refs[28:36]
+    send, recv, local = refs[36:39]
     me, place = lax.axis_index("narrow"), lax.axis_index("wide")
     x_peer = me + 1 - 2 * (me % 2)
     y_peer = (me + 2) % 4
@@ -170,7 +161,7 @@
     chunks = width // TILE
     parts = 4 * (units // TILE)
 
-    sizes = [2] + [parts] * 4 + [chunks] * 4 + [units // TILE] + [chunks] * 4
+    sizes = [2] + [parts] * 4 + [chunks] * 4 + [units // TILE] + [chunks] * 4 + [chunks] * (replicas - 1)
     starts = [sum(sizes[:k]) for k in range(len(sizes) + 1)]
 
     def link(kind, index, src, dst, axis, peer):
@@ -236,11 +227,21 @@
     def relay_by_x(c):
         return link(13, c, slot(2, c), slot(3, c), "narrow", x_peer)
 
+    kept_t = TILE // SPAN * BAND
+
+    def band_rows(c):
+        return pl.ds(pl.multiple_of(c * kept_t, kept_t), kept_t)
+
+    def band_copy(k, c):
+        mine = bands.at[place, band_rows(c)]
+        return link(14 + k, c, mine, mine, "wide", others[k])
+
     def load(k, src, dst):
         return pltpu.make_async_copy(src, dst, local.at[k])
 
     barrier = pltpu.get_barrier_semaphore()
-    for axis, peer in (("narrow", x_peer), ("narrow", y_peer), ("wide", twin), ("wide", z_peer)):
+    others = [(place + k) % replicas for k in range(1, replicas)]
+    for axis, peer in [("narrow", x_peer), ("narrow", y_peer)] + [("wide", p) for p in others]:
         pl.semaphore_signal(
             barrier, inc=1, device_id={axis: peer}, device_id_type=pl.DeviceIdType.MESH
         )
@@ -255,7 +256,7 @@
     loads += [load(6 + k, s, d) for k, (s, d) in enumerate(zip(tables_hbm, tables_vmem))]
     for copy in loads:
         copy.start()
-    pl.semaphore_wait(barrier, 4)
+    pl.semaphore_wait(barrier, 1 + replicas)
     for k in range(2):
         token_copy(k).start()
     for k in range(parts):
@@ -337,7 +338,10 @@
             state.at[:, cols(c)], residue_hbm.at[0, :, cols(c)], local.at[14 + c]
         )
 
-    kept_t = TILE // SPAN * BAND
+    def store_update(c):
+        return pltpu.make_async_copy(
+            update.at[:, cols(c)], update_hbm.at[:, cols(c)], local.at[14 + chunks + c]
+        )
 
     def gradient(c):
         @pl.when(c % 3 != 2)
@@ -354,9 +358,21 @@
         table = tables()
         squeezed = dot3(table[0], halves(moved), (1, 0))
         band = dot3(halves(squeezed), table[2], (1, 0))
-        band_t[pl.ds(pl.multiple_of(c * kept_t, kept_t), kept_t), :] = band.T
+        bands[place, band_rows(c), :] = band.T.astype(BF)
+        for k in range(replicas - 1):
+            band_copy(k, c).start()
         state[:, cols(c)] = moved - decode_tile(band, table)
         store(c).start()
+
+    def shared(c):
+        for k in range(replicas - 1):
+            band_copy(k, c).wait_recv()
+        total = bands[0, band_rows(c), :].astype(F32)
+        for k in range(1, replicas):
+            total = total + bands[k, band_rows(c), :].astype(F32)
+        tile = decode_tile(total.T, tables()) * (1.0 / replicas)
+        update[:, cols(c)] = tile.astype(BF)
+        store_update(c).start()
 
     for k in range(3):
         loads[k].wait()
@@ -400,7 +416,7 @@
 
     lag = 3
 
-    @pl.loop(0, chunks + lag)
+    @pl.loop(0, chunks + lag + 1)
     def _(c):
         @pl.when(c < chunks)
         def _():
@@ -428,9 +444,13 @@
             for t in range(units // TILE):
                 lend_copy(t).wait_recv()
 
-        @pl.when(c >= lag)
+        @pl.when((c >= lag) & (c < chunks + lag))
         def _():
             gradient(c - lag)
+
+        @pl.when(c > lag)
+        def _():
+            shared(c - lag - 1)
 
     for k in range(2):
         token_copy(k).wait_send()
@@ -448,10 +468,13 @@
         error_x(c).wait_send()
         error_y(c).wait_send()
         relay_by_y(c).wait_send()
+        for k in range(replicas - 1):
+            band_copy(k, c).wait_send()
         store(c).wait()
-
-
-def split_step(tokens, target, combine, filled, w_gate, w_up, w_down, momentum, tables, factor):
+        store_update(c).wait()
+
+
+def split_step(tokens, target, combine, filled, w_gate, w_up, w_down, momentum, tables, factor, replicas):
     rows, width = tokens.shape
     units = w_down.shape[0]
     vmem = pl.BlockSpec(memory_space=pltpu.VMEM)
@@ -459,14 +482,14 @@
     block = lambda *shape: pltpu.VMEM(shape, BF)
     chunks = width // TILE
     tiles = units // TILE
-    count = 2 + 16 * tiles + 8 * chunks + tiles
+    count = 2 + 16 * tiles + 8 * chunks + tiles + (replicas - 1) * chunks
     return pl.pallas_call(
-        functools.partial(split_kernel, factor),
+        functools.partial(split_kernel, factor, replicas),
         in_specs=[hbm, hbm, vmem, pl.BlockSpec(memory_space=pltpu.SMEM)] + [hbm] * 12,
-        out_specs=[hbm, vmem],
+        out_specs=[hbm, hbm],
         out_shape=[
             jax.ShapeDtypeStruct((1, units, width), F32),
-            jax.ShapeDtypeStruct((width // SPAN * BAND, units // SPAN * BAND), F32),
+            jax.ShapeDtypeStruct((units, width), BF),
         ],
         scratch_shapes=[
             block(2 * rows, width), block(rows, width), pltpu.VMEM((rows, 128), F32),
@@ -474,11 +497,12 @@
             block(2 * units, width), block(2 * rows, 2 * units), block(units, 4 * rows),
             block(units, 2 * rows), pltpu.VMEM((rows, width), F32), block(rows, width),
             block(rows, width), block(4 * rows, width), pltpu.VMEM((units, width), F32),
+            block(replicas, width // SPAN * BAND, units // SPAN * BAND), block(units, width),
         ]
         + [block(*t.shape) for t in tables]
         + [
             pltpu.SemaphoreType.DMA((count,)), pltpu.SemaphoreType.DMA((count,)),
-            pltpu.SemaphoreType.DMA((14 + chunks,)),
+            pltpu.SemaphoreType.DMA((14 + 2 * chunks,)),
         ],
         compiler_params=pltpu.CompilerParams(
             collective_id=0, has_side_effects=True, vmem_limit_bytes=60 << 20
@@ -487,55 +511,6 @@
     )(
         tokens, target, combine.reshape(1, rows), filled, w_gate, w_up, w_down, momentum, *tables
     )
-
-
-def band_kernel(count, band, total, outgoing, arrived, summed, gathered, send, recv):
-    me = lax.axis_index("wide")
-    peers = [(me + k) % count for k in range(1, count)]
-    greet("wide", peers)
-    share = band.shape[0] // count
-    outgoing[...] = band[...].reshape(count, share, band.shape[1]).astype(BF)
-    first = [
-        remote(outgoing.at[p], arrived.at[k], send, recv, k, "wide", p)
-        for k, p in enumerate(peers)
-    ]
-    for copy in first:
-        copy.start()
-    amount = outgoing[me].astype(F32)
-    for k, copy in enumerate(first):
-        copy.wait_recv()
-        amount = amount + arrived[k].astype(F32)
-    summed[...] = amount.astype(BF)
-    second = [
-        remote(summed, gathered.at[me], send, recv, count + k, "wide", p)
-        for k, p in enumerate(peers)
-    ]
-    for copy in second:
-        copy.start()
-    for copy in second:
-        copy.wait_recv()
-    for copy in first + second:
-        copy.wait_send()
-    gathered[me] = summed[...]
-    total[...] = gathered[...].astype(F32).reshape(band.shape)
-
-
-def band_sum(band, count):
-    share = band.shape[0] // count
-    vmem = pl.BlockSpec(memory_space=pltpu.VMEM)
-    block = lambda *shape: pltpu.VMEM(shape + (share, band.shape[1]), BF)
-    return pl.pallas_call(
-        functools.partial(band_kernel, count),
-        in_specs=[vmem],
-        out_specs=vmem,
-        out_shape=jax.ShapeDtypeStruct(band.shape, F32),
-        scratch_shapes=[
-            block(count), block(count - 1), block(), block(count),
-            pltpu.SemaphoreType.DMA((2 * count,)), pltpu.SemaphoreType.DMA((2 * count,)),
-        ],
-        compiler_params=pltpu.CompilerParams(collective_id=1, has_side_effects=True),
-        name="band_sum",
-    )(band)
 
 
 def forward(tokens, target, combine, filled, w_gate, w_up, w_down):
@@ -566,15 +541,14 @@
     factor = 1.0 / math.sqrt(total_rows)
     fits = units == 2 * TILE and width % TILE == 0 and tokens.shape[0] % 128 == 0
     if narrow == 4 and replicas % 4 == 0 and fits:
-        residue, band = split_step(
-            tokens, target, combine, filled, w_gate, w_up, w_down, momentum, tables, factor
+        return split_step(
+            tokens, target, combine, filled, w_gate, w_up, w_down, momentum, tables, factor,
+            replicas,
         )
-        total = band_sum(band, replicas)
-    else:
-        hidden_t, errors = forward(tokens, target, combine, filled, w_gate, w_up, w_down)
-        residue, band = grad_step(hidden_t, errors, momentum, tables, factor)
-        bands = lax.all_gather(band.astype(BF)[None], "wide", axis=0, tiled=True)
-        total = jnp.sum(bands.astype(F32), axis=0)
+    hidden_t, errors = forward(tokens, target, combine, filled, w_gate, w_up, w_down)
+    residue, band = grad_step(hidden_t, errors, momentum, tables, factor)
+    bands = lax.all_gather(band.astype(BF)[None], "wide", axis=0, tiled=True)
+    total = jnp.sum(bands.astype(F32), axis=0)
     return residue, update_step(total, tables, units, width, replicas)
 
 

time: 140 us -> 131 us (0.936)
  Pallas kernels: 132 us -> 122 us
  local copies, waits for them, and re-layouts: 6.05 us -> 7.61 us
    pallas_call x3 -> x1, Pallas kernels: 132 us -> 122 us  [split_step(): pl.pallas_call(functools.partial(split_kernel, factor, replicas), in_spec...]
    unnamed x1 -> x4, local copies, waits for them, and re-layouts: 4.82 us -> 6.39 us
where the time goes in v2:
time: 131 us
  Pallas kernels  122 us (93%)
  local copies, waits for them, and re-layouts  7.61 us (6%)
    pallas_call x1, Pallas kernels, split_step(): pl.pallas_call(functools.partial(split_kernel, factor, replicas), in_spec...  122 us
    unnamed x4, local copies, waits for them, and re-layouts  6.39 us

profile of v2, /device:TPU:0, one launch (start us, length us, event | category | flops | bytes accessed | tf_op | source)
XLA Modules:
  0.0 131.2 jit_solution(15415451290854574505)
XLA Ops:
  1.3 1.2 reshape.7.combine
  2.5 122.3 %split_step.1 = (f32[1,512,2304]{2,1,0:T(8,128)}, bf16[512,2304]{1,0:T(8,128)(2,1)}) custom-call(bf16[256,2304]{1,0:T(8,128)(2,1)} %tokens_hbm.1, bf16[256,2304]{1,0:T(8,128)(2,1)} %target_hbm.1, bf16[1,256]{1,0:T(2,128)(2,1)} %reshape.7.combine, s32[1]{0:T(128)S(6)} %copy.20.filled, bf16[2304,512]{1,0:T(8,128)(2,1)} %gate_hbm.1, bf16[2304,512]{1,0:T(8,128)(2,1)} %up_hbm.1, ...), custom_call_target="tpu_custom_call" | custom-call | tf_op jit(solution)/shard_map/split_step/pallas_call | solution.py:486
  124.8 0.0 copy-start
  124.8 5.0 %copy.21 = f32[1,512,2304]{2,1,0:T(8,128)} copy(f32[1,512,2304]{2,1,0:T(8,128)} %get-tuple-element.4) | data formatting | bytes 9437184
  129.7 0.0 copy-done
  129.8 1.4 %copy.22 = bf16[512,2304]{1,0:T(8,128)(2,1)} copy(bf16[512,2304]{1,0:T(8,128)(2,1)S(1)} %copy-done) | data formatting | bytes 4718592
Async XLA Ops:
  124.8 5.0 %copy-start = (bf16[512,2304]{1,0:T(8,128)(2,1)S(1)}, bf16[512,2304]{1,0:T(8,128)(2,1)}, u32[]{:S(2)}) copy-start(bf16[512,2304]{1,0:T(8,128)(2,1)} %get-tuple-element.5) | copy-start | bytes 7077892

commit v3 on v2

v3 whole, which is shorter than its diff:
```python
import functools
import math

import jax
import jax.numpy as jnp
import numpy as np
from jax import lax
from jax.experimental import pallas as pl
from jax.experimental.pallas import tpu as pltpu
from jax.sharding import PartitionSpec as P

SPAN = 64
BAND = 16
TILE = 256
CUTS = 4
BF = jnp.bfloat16
F32 = jnp.float32


def block_table(blocks):
    row = np.arange(blocks * BAND)[:, None]
    col = np.arange(blocks * SPAN)[None, :]
    factor = np.where(row % BAND == 0, math.sqrt(1.0 / SPAN), math.sqrt(2.0 / SPAN))
    value = factor * np.cos(math.pi * (2.0 * (col % SPAN) + 1.0) * (row % BAND) / (2.0 * SPAN))
    return np.where(row // BAND == col // SPAN, value, 0.0).astype(np.float32)


def halves(value):
    high = value.astype(BF)
    return high, (value - high.astype(F32)).astype(BF)


def dot3(left, right, contract):
    dims = (((contract[0],), (contract[1],)), ((), ()))
    dot = functools.partial(lax.dot_general, dimension_numbers=dims, preferred_element_type=F32)
    return dot(left[0], right[0]) + (dot(left[1], right[0]) + dot(left[0], right[1]))


def decode_tile(band, tables):
    wide = dot3(halves(band), tables[3], (1, 0))
    return dot3(tables[1], halves(wide), (1, 0))


def read_tables(refs):
    return [(refs[2 * k][...], refs[2 * k + 1][...]) for k in range(4)]


def grad_kernel(factor, subs, hidden_t, error, momentum, *refs):
    residue, band_t = refs[8:]
    tables = read_tables(refs)
    kept_t = TILE // SPAN * BAND
    for k in range(subs):
        at = slice(k * TILE, (k + 1) * TILE)
        grad = jnp.dot(hidden_t[...], error[:, at], preferred_element_type=F32)
        moved = 0.999 * momentum[0, :, at] + factor * grad
        squeezed = dot3(tables[0], halves(moved), (1, 0))
        band = dot3(halves(squeezed), tables[2], (1, 0))
        band_t[k * kept_t : (k + 1) * kept_t, :] = band.T
        residue[0, :, at] = moved - decode_tile(band, tables)


def whole(a):
    return pl.BlockSpec(a.shape, lambda i: (0,) * a.ndim)


def grad_step(hidden_t, error, momentum, tables, factor):
    units, rows = hidden_t.shape
    width = error.shape[1]
    subs = 3 if width // TILE % 3 == 0 else 1
    step = TILE * subs
    tiles = width // step
    kept = units // SPAN * BAND
    kept_t = step // SPAN * BAND
    return pl.pallas_call(
        functools.partial(grad_kernel, factor, subs),
        grid=(tiles,),
        in_specs=[
            whole(hidden_t),
            pl.BlockSpec((rows, step), lambda i: (0, i)),
            pl.BlockSpec((1, units, step), lambda i: (0, 0, i)),
        ]
        + [whole(t) for t in tables],
        out_specs=[
            pl.BlockSpec((1, units, step), lambda i: (0, 0, i)),
            pl.BlockSpec((kept_t, kept), lambda i: (i, 0)),
        ],
        out_shape=[
            jax.ShapeDtypeStruct((1, units, width), F32),
            jax.ShapeDtypeStruct((tiles * kept_t, kept), F32),
        ],
        name="grad_step",
    )(hidden_t, error, momentum, *tables)


def update_kernel(replicas, subs, bands, *refs):
    update = refs[8]
    tables = read_tables(refs)
    kept_t = TILE // SPAN * BAND
    for k in range(subs):
        band = bands[k * kept_t : (k + 1) * kept_t, :].T
        tile = decode_tile(band, tables) * (1.0 / replicas)
        update[:, k * TILE : (k + 1) * TILE] = tile.astype(BF)


def update_step(bands, tables, units, width, replicas):
    rows_t, kept = bands.shape
    subs = 3 if width // TILE % 3 == 0 else 1
    step = TILE * subs
    tiles = width // step
    return pl.pallas_call(
        functools.partial(update_kernel, replicas, subs),
        grid=(tiles,),
        in_specs=[pl.BlockSpec((rows_t // tiles, kept), lambda i: (i, 0))]
        + [whole(t) for t in tables],
        out_specs=pl.BlockSpec((units, step), lambda i: (0, i)),
        out_shape=jax.ShapeDtypeStruct((units, width), BF),
        name="update_step",
    )(bands, *tables)


def make_tables(units):
    left = block_table(units // SPAN)
    right = block_table(TILE // SPAN)
    pieces = []
    for table in (left, left.T, right.T, right):
        high = table.astype(BF)
        pieces += [high, (table - high.astype(np.float32)).astype(BF)]
    return [jnp.asarray(np.ascontiguousarray(p)) for p in pieces]


def remote(src, dst, send, recv, index, axis, peer):
    return pltpu.make_async_remote_copy(
        src_ref=src,
        dst_ref=dst,
        send_sem=send.at[index],
        recv_sem=recv.at[index],
        device_id={axis: peer},
        device_id_type=pl.DeviceIdType.MESH,
    )


def split_kernel(
    factor, replicas, tokens_hbm, target_hbm, combine_hbm, filled, gate_hbm, up_hbm, down_hbm,
    momentum_hbm, *refs
):
    tables_hbm, (residue_hbm, update_hbm) = refs[:8], refs[8:10]
    (
        tok, target, combine, combine_x, weight, gate, up, gate_y, up_y, down, hidden, hidden_t,
        kept, sent, came, lent, given, state, bands, update,
    ) = refs[10:30]
    tables_vmem = refs[30:38]
    send, recv, local = refs[38:41]
    me, place = lax.axis_index("narrow"), lax.axis_index("wide")
    x_peer = me + 1 - 2 * (me % 2)
    y_peer = (me + 2) % 4
    twin = place + 1 - 2 * (place % 2)
    z_peer = place + 2 - 4 * (place // 2 % 2)
    others = [(place + k) % replicas for k in range(1, replicas)]
    quarter = place % 4
    rows, width = target.shape
    units = gate.shape[1]
    deep, flat = width // 4, units // 4
    cut = deep // CUTS
    chunks = width // TILE
    tiles = units // TILE
    parts = 2 * CUTS * tiles

    sizes = [2, 1] + [parts] * 4 + [chunks] * (7 + replicas - 1)
    starts = [sum(sizes[:k]) for k in range(len(sizes) + 1)]

    def link(kind, index, src, dst, axis, peer):
        return remote(src, dst, send, recv, starts[kind] + index, axis, peer)

    def cols(c):
        if isinstance(c, int):
            return pl.ds(c * TILE, TILE)
        return pl.ds(pl.multiple_of(c * TILE, TILE), TILE)

    def token_copy(k):
        part = rows // 2
        src = tokens_hbm.at[pl.ds(k * part, part)]
        return link(0, k, src, tok.at[pl.ds(rows + k * part, part)], "narrow", x_peer)

    def combine_copy():
        return link(1, 0, combine_hbm, combine_x, "narrow", x_peer)

    def piece(k, ref, owner):
        first = pl.multiple_of(owner * deep + k % CUTS * cut, 16)
        return ref.at[pl.ds(first, cut), cols(k // (2 * CUTS))]

    def weight_copy(kind, k):
        mine, theirs = ((gate_hbm, gate_y), (up_hbm, up_y))[k // CUTS % 2]
        if kind == 2:
            return link(2, k, piece(k, mine, quarter), piece(k, theirs, quarter), "narrow", y_peer)
        if kind == 5:
            there = piece(k, theirs, (quarter + 2) % 4)
            return link(5, k, there, there, "wide", twin)
        here = piece(k, theirs, quarter)
        return link(kind, k, here, here, "wide", z_peer if kind == 3 else twin)

    def down_piece(c, ref, first, owner):
        return ref.at[pl.ds(pl.multiple_of(first + owner * flat, 16), flat), cols(c)]

    def down_copy(kind, c):
        if kind == 6:
            src = down_piece(c, down_hbm, 0, quarter)
            return link(6, c, src, down_piece(c, down, units, quarter), "narrow", y_peer)
        if kind == 9:
            there = down_piece(c, down, units, (quarter + 2) % 4)
            return link(9, c, there, there, "wide", twin)
        here = down_piece(c, down, units, quarter)
        return link(kind, c, here, here, "wide", z_peer if kind == 7 else twin)

    def half_copy(k, c):
        src, dst = sent.at[pl.ds(k * rows, rows), cols(c)], came.at[pl.ds(k * rows, rows), cols(c)]
        return link(10 + k, c, src, dst, "narrow", x_peer)

    def grad_copy(c):
        return link(12, c, lent.at[:, cols(c)], given.at[:, cols(c)], "narrow", y_peer)

    kept_t = TILE // SPAN * BAND

    def band_rows(c):
        return pl.ds(pl.multiple_of(c * kept_t, kept_t), kept_t)

    def band_copy(k, c):
        mine = bands.at[place, band_rows(c)]
        return link(13 + k, c, mine, mine, "wide", others[k])

    def load(k, src, dst):
        return pltpu.make_async_copy(src, dst, local.at[k])

    def store(c):
        return load(15 + c, state.at[:, cols(c)], residue_hbm.at[0, :, cols(c)])

    def store_update(c):
        return load(15 + chunks + c, update.at[:, cols(c)], update_hbm.at[:, cols(c)])

    barrier = pltpu.get_barrier_semaphore()
    for axis, peer in [("narrow", x_peer), ("narrow", y_peer)] + [("wide", p) for p in others]:
        pl.semaphore_signal(
            barrier, inc=1, device_id={axis: peer}, device_id_type=pl.DeviceIdType.MESH
        )
    loads = [
        load(0, tokens_hbm, tok.at[pl.ds(0, rows)]),
        load(1, gate_hbm, gate),
        load(2, up_hbm, up),
        load(3, combine_hbm, combine),
        load(4, down_hbm, down.at[pl.ds(0, units)]),
        load(5, target_hbm, target),
        load(6, momentum_hbm.at[0], state),
    ]
    loads += [load(7 + k, s, d) for k, (s, d) in enumerate(zip(tables_hbm, tables_vmem))]
    for copy in loads:
        copy.start()
    pl.semaphore_wait(barrier, 1 + replicas)
    combine_copy().start()
    for k in range(2):
        token_copy(k).start()
    for k in range(parts):
        weight_copy(2, k).start()

    @pl.loop(0, chunks)
    def _(c):
        down_copy(6, c).start()

    def expert(first, count, gates, ups, base, t):
        block = tok[first : first + count, :]
        gated = jnp.dot(block, gates[:, cols(t)], preferred_element_type=F32)
        raised = jnp.dot(block, ups[:, cols(t)], preferred_element_type=F32)
        value = gated / (1.0 + jnp.exp(-gated)) * raised
        at = slice(base + t * TILE, base + (t + 1) * TILE)
        hidden[first : first + count, at] = value.astype(BF)
        hidden_t[at, first : first + count] = value.T.astype(BF)

    def pass_weight(k):
        weight_copy(2, k).wait_recv()
        weight_copy(3, k).start()
        weight_copy(4, k).start()

    def share_weight(k):
        weight_copy(3, k).wait_recv()
        weight_copy(5, k).start()

    def take_weights(first, last):
        for k in range(first, last):
            weight_copy(4, k).wait_recv()
            weight_copy(5, k).wait_recv()

    def pass_down(c):
        down_copy(6, c).wait_recv()
        down_copy(7, c).start()
        down_copy(8, c).start()

    def share_down(c):
        down_copy(7, c).wait_recv()
        down_copy(9, c).start()

    def take_down(c):
        down_copy(8, c).wait_recv()
        down_copy(9, c).wait_recv()

    def wide_weight(k):
        return jnp.concatenate([weight[k]] * (TILE // weight.shape[2]), axis=1)

    def peer_half(c):
        part = jnp.dot(hidden[rows:, :], down[:, cols(c)], preferred_element_type=F32)
        sent[rows:, cols(c)] = part.astype(BF)
        half_copy(1, c).start()
        scale = wide_weight(1)
        kept[rows:, cols(c)] = scale * (scale * part)

    def own_half(c):
        part = jnp.dot(hidden[:rows, :], down[:, cols(c)], preferred_element_type=F32)
        scale = wide_weight(0)
        value = scale * (scale * part - target[:, cols(c)].astype(F32))
        sent[:rows, cols(c)] = value.astype(BF)
        half_copy(0, c).start()
        kept[:rows, cols(c)] = value

    def lend(c):
        half_copy(1, c).wait_recv()
        scale = wide_weight(0)
        mine = kept[:rows, cols(c)] + scale * (scale * came[rows:, cols(c)].astype(F32))
        half_copy(0, c).wait_recv()
        theirs = kept[rows:, cols(c)] + came[:rows, cols(c)].astype(F32)
        error = jnp.concatenate([mine.astype(BF), theirs.astype(BF)], axis=0)
        grad = jnp.dot(hidden_t[units:, :], error, preferred_element_type=F32)
        lent[:, cols(c)] = (factor * grad).astype(BF)
        grad_copy(c).start()
        grad = jnp.dot(hidden_t[:units, :], error, preferred_element_type=F32)
        state[:, cols(c)] = 0.999 * state[:, cols(c)] + factor * grad

    tables = lambda: [(tables_vmem[2 * k][...], tables_vmem[2 * k + 1][...]) for k in range(4)]

    def gradient(c):
        grad_copy(c).wait_recv()
        moved = state[:, cols(c)] + given[:, cols(c)].astype(F32)
        table = tables()
        squeezed = dot3(table[0], halves(moved), (1, 0))
        band = dot3(halves(squeezed), table[2], (1, 0))
        bands[place, band_rows(c), :] = band.T.astype(BF)
        for k in range(replicas - 1):
            band_copy(k, c).start()
        state[:, cols(c)] = moved - decode_tile(band, table)
        store(c).start()

    def shared(c):
        for k in range(replicas - 1):
            band_copy(k, c).wait_recv()
        total = bands[0, band_rows(c), :].astype(F32)
        for k in range(1, replicas):
            total = total + bands[k, band_rows(c), :].astype(F32)
        tile = decode_tile(total.T, tables()) * (1.0 / replicas)
        update[:, cols(c)] = tile.astype(BF)
        store_update(c).start()

    for k in range(3):
        loads[k].wait()
    for t in range(tiles):
        expert(0, rows, gate, up, 0, t)
    first = parts // 2
    behind = 2
    for k in range(first + behind):
        pass_weight(k)
        if k >= behind:
            share_weight(k - behind)
    take_weights(0, first)
    expert(0, rows, gate_y, up_y, units, 0)
    for k in range(first + behind, parts - 1):
        share_weight(k - behind)
        pass_weight(k)
    share_weight(parts - 1 - behind)
    loads[3].wait()
    combine_copy().wait_recv()
    for k, (owner, ref) in enumerate(((me, combine), (x_peer, combine_x))):
        row_ids = owner * rows + lax.broadcasted_iota(jnp.int32, (1, rows), 1)
        value = ref[...].astype(F32).reshape(1, rows)
        live = jnp.where(row_ids < filled[0], value, 0.0)
        weight[k] = jnp.broadcast_to(live, (weight.shape[2], rows)).T
    for k in range(2):
        token_copy(k).wait_recv()
    expert(rows, rows, gate, up, 0, 0)
    pass_weight(parts - 1)
    share_weight(parts - behind)
    expert(rows, rows, gate, up, 0, 1)
    pass_down(0)
    expert(rows, rows, gate_y, up_y, units, 0)
    share_weight(parts - 1)
    pass_down(1)
    take_weights(first, parts)
    expert(rows, rows, gate_y, up_y, units, 1)
    for copy in loads[4:]:
        copy.wait()
    pass_down(2)
    share_down(0)
    take_down(0)
    peer_half(0)
    expert(0, rows, gate_y, up_y, units, 1)
    own_half(0)
    share_down(1)
    pass_down(3)
    take_down(1)
    peer_half(1)
    own_half(1)
    share_down(2)

    lag = 2

    @pl.loop(0, chunks + lag + 1)
    def _(c):
        @pl.when(c < chunks)
        def _():
            lend(c)

        @pl.when(c + 4 < chunks)
        def _():
            pass_down(c + 4)

        @pl.when(c + 3 < chunks)
        def _():
            share_down(c + 3)

        @pl.when(c + 2 < chunks)
        def _():
            take_down(c + 2)
            peer_half(c + 2)
            own_half(c + 2)

        @pl.when((c >= lag) & (c < chunks + lag))
        def _():
            gradient(c - lag)

        @pl.when(c > lag)
        def _():
            shared(c - lag - 1)

    combine_copy().wait_send()
    for k in range(2):
        token_copy(k).wait_send()
    for k in range(parts):
        for kind in range(2, 6):
            weight_copy(kind, k).wait_send()

    @pl.loop(0, chunks)
    def _(c):
        for kind in range(6, 10):
            down_copy(kind, c).wait_send()
        for k in range(2):
            half_copy(k, c).wait_send()
        grad_copy(c).wait_send()
        for k in range(replicas - 1):
            band_copy(k, c).wait_send()
        store(c).wait()
        store_update(c).wait()


def split_step(
    tokens, target, combine, filled, w_gate, w_up, w_down, momentum, tables, factor, replicas
):
    rows, width = tokens.shape
    units = w_down.shape[0]
    hbm = pl.BlockSpec(memory_space=pl.ANY)
    block = lambda *shape: pltpu.VMEM(shape, BF)
    chunks = width // TILE
    count = 3 + 8 * CUTS * (units // TILE) + (6 + replicas) * chunks
    return pl.pallas_call(
        functools.partial(split_kernel, factor, replicas),
        in_specs=[hbm] * 3 + [pl.BlockSpec(memory_space=pltpu.SMEM)] + [hbm] * 12,
        out_specs=[hbm, hbm],
        out_shape=[
            jax.ShapeDtypeStruct((1, units, width), F32),
            jax.ShapeDtypeStruct((units, width), BF),
        ],
        scratch_shapes=[
            block(2 * rows, width), block(rows, width), block(rows), block(rows),
            pltpu.VMEM((2, rows, 128), F32),
            block(width, units), block(width, units), block(width, units), block(width, units),
            block(2 * units, width), block(2 * rows, 2 * units), block(2 * units, 2 * rows),
            pltpu.VMEM((2 * rows, width), F32), block(2 * rows, width), block(2 * rows, width),
            block(units, width), block(units, width), pltpu.VMEM((units, width), F32),
            block(replicas, width // SPAN * BAND, units // SPAN * BAND), block(units, width),
        ]
        + [block(*t.shape) for t in tables]
        + [
            pltpu.SemaphoreType.DMA((count,)), pltpu.SemaphoreType.DMA((count,)),
            pltpu.SemaphoreType.DMA((15 + 2 * chunks,)),
        ],
        compiler_params=pltpu.CompilerParams(
            collective_id=0, has_side_effects=True, vmem_limit_bytes=60 << 20
        ),
        name="split_step",
    )(tokens, target, combine, filled, w_gate, w_up, w_down, momentum, *tables)


def forward(tokens, target, combine, filled, w_gate, w_up, w_down):
    local_rows = tokens.shape[0]
    piece = lax.all_gather(tokens, "narrow", axis=0, tiled=True)
    gate_proj = jnp.dot(piece, w_gate, preferred_element_type=F32)
    up_proj = jnp.dot(piece, w_up, preferred_element_type=F32)
    hidden = (jax.nn.silu(gate_proj) * up_proj).astype(BF)
    summed = lax.psum_scatter(
        jnp.dot(hidden, w_down, preferred_element_type=F32).astype(BF),
        "narrow",
        scatter_dimension=0,
        tiled=True,
    ).astype(F32)
    weight = combine.astype(F32)[:, None]
    row_ids = lax.axis_index("narrow") * local_rows + jnp.arange(local_rows, dtype=jnp.int32)
    error = jnp.where(
        (row_ids < filled[0])[:, None], weight * (weight * summed - target.astype(F32)), 0.0
    ).astype(BF)
    return hidden.T, lax.all_gather(error, "narrow", axis=0, tiled=True)


def body(tokens, target, combine, filled, w_gate, w_up, w_down, momentum):
    units, width = w_down.shape
    narrow, replicas = lax.axis_size("narrow"), lax.axis_size("wide")
    total_rows = tokens.shape[0] * narrow
    tables = make_tables(units)
    factor = 1.0 / math.sqrt(total_rows)
    fits = units == 2 * TILE and width % (64 * CUTS) == 0 and tokens.shape[0] % 128 == 0
    if narrow == 4 and replicas % 4 == 0 and fits:
        return split_step(
            tokens, target, combine, filled, w_gate, w_up, w_down, momentum, tables, factor,
            replicas,
        )
    hidden_t, errors = forward(tokens, target, combine, filled, w_gate, w_up, w_down)
    residue, band = grad_step(hidden_t, errors, momentum, tables, factor)
    bands = lax.all_gather(band.astype(BF)[None], "wide", axis=0, tiled=True)
    total = jnp.sum(bands.astype(F32), axis=0)
    return residue, update_step(total, tables, units, width, replicas)


def solution(mesh):
    in_specs = (
        P(("wide", "narrow"), None),
        P(("wide", "narrow"), None),
        P(("wide", "narrow")),
        P("wide"),
        P(None, "narrow"),
        P(None, "narrow"),
        P("narrow", None),
        P("wide", "narrow", None),
    )
    out_specs = (P("wide", "narrow", None), P("narrow", None))
    return jax.shard_map(body, mesh=mesh, in_specs=in_specs, out_specs=out_specs, check_vma=False)
```

time: 131 us -> 122 us (0.931)
  Pallas kernels: 122 us -> 114 us
    pallas_call x1, Pallas kernels: 122 us -> 114 us  [split_step(): pl.pallas_call(functools.partial(split_kernel, factor, replicas), in_spec...]
where the time goes in v3:
time: 122 us
  Pallas kernels  114 us (93%)
  local copies, waits for them, and re-layouts  6.39 us (5%)
  between operations  1.29 us (1%)
    pallas_call x1, Pallas kernels, split_step(): pl.pallas_call(functools.partial(split_kernel, factor, replicas), in_spec...  114 us
    unnamed x4, local copies, waits for them, and re-layouts  6.39 us

profile of v3, /device:TPU:0, one launch (start us, length us, event | category | flops | bytes accessed | tf_op | source)
XLA Modules:
  0.0 122.1 jit_solution(10382379782000238685)
XLA Ops:
  1.3 114.4 %split_step.1 = (f32[1,512,2304]{2,1,0:T(8,128)}, bf16[512,2304]{1,0:T(8,128)(2,1)}) custom-call(bf16[256,2304]{1,0:T(8,128)(2,1)} %tokens_hbm.1, bf16[256,2304]{1,0:T(8,128)(2,1)} %target_hbm.1, bf16[256]{0:T(256)(128)(2,1)} %combine_hbm.1, s32[1]{0:T(128)S(6)} %copy.20.filled, bf16[2304,512]{1,0:T(8,128)(2,1)} %gate_hbm.1, bf16[2304,512]{1,0:T(8,128)(2,1)} %up_hbm.1, ...), custom_call_target="tpu_custom_call" | custom-call | tf_op jit(solution)/shard_map/split_step/pallas_call | solution.py:467
  115.7 0.0 copy-start
  115.7 5.0 %copy.21 = f32[1,512,2304]{2,1,0:T(8,128)} copy(f32[1,512,2304]{2,1,0:T(8,128)} %get-tuple-element.4) | data formatting | bytes 9437184
  120.7 0.0 copy-done
  120.7 1.4 %copy.22 = bf16[512,2304]{1,0:T(8,128)(2,1)} copy(bf16[512,2304]{1,0:T(8,128)(2,1)S(1)} %copy-done) | data formatting | bytes 4718592
Async XLA Ops:
  115.7 5.0 %copy-start = (bf16[512,2304]{1,0:T(8,128)(2,1)S(1)}, bf16[512,2304]{1,0:T(8,128)(2,1)}, u32[]{:S(2)}) copy-start(bf16[512,2304]{1,0:T(8,128)(2,1)} %get-tuple-element.5) | copy-start | bytes 7077892

commit v4 on v3

--- a/solution.py
+++ b/solution.py
@@ -143,13 +143,13 @@
     factor, replicas, tokens_hbm, target_hbm, combine_hbm, filled, gate_hbm, up_hbm, down_hbm,
     momentum_hbm, *refs
 ):
-    tables_hbm, (residue_hbm, update_hbm) = refs[:8], refs[8:10]
+    tables_hbm, (state, update) = refs[:8], refs[8:10]
     (
         tok, target, combine, combine_x, weight, gate, up, gate_y, up_y, down, hidden, hidden_t,
-        kept, sent, came, lent, given, state, bands, update,
-    ) = refs[10:30]
-    tables_vmem = refs[30:38]
-    send, recv, local = refs[38:41]
+        kept, sent, came, lent, given, bands,
+    ) = refs[10:28]
+    tables_vmem = refs[28:36]
+    send, recv, local = refs[36:39]
     me, place = lax.axis_index("narrow"), lax.axis_index("wide")
     x_peer = me + 1 - 2 * (me % 2)
     y_peer = (me + 2) % 4
@@ -230,12 +230,6 @@
     def load(k, src, dst):
         return pltpu.make_async_copy(src, dst, local.at[k])
 
-    def store(c):
-        return load(15 + c, state.at[:, cols(c)], residue_hbm.at[0, :, cols(c)])
-
-    def store_update(c):
-        return load(15 + chunks + c, update.at[:, cols(c)], update_hbm.at[:, cols(c)])
-
     barrier = pltpu.get_barrier_semaphore()
     for axis, peer in [("narrow", x_peer), ("narrow", y_peer)] + [("wide", p) for p in others]:
         pl.semaphore_signal(
@@ -248,7 +242,7 @@
         load(3, combine_hbm, combine),
         load(4, down_hbm, down.at[pl.ds(0, units)]),
         load(5, target_hbm, target),
-        load(6, momentum_hbm.at[0], state),
+        load(6, momentum_hbm, state),
     ]
     loads += [load(7 + k, s, d) for k, (s, d) in enumerate(zip(tables_hbm, tables_vmem))]
     for copy in loads:
@@ -329,21 +323,20 @@
         lent[:, cols(c)] = (factor * grad).astype(BF)
         grad_copy(c).start()
         grad = jnp.dot(hidden_t[:units, :], error, preferred_element_type=F32)
-        state[:, cols(c)] = 0.999 * state[:, cols(c)] + factor * grad
+        state[0, :, cols(c)] = 0.999 * state[0, :, cols(c)] + factor * grad
 
     tables = lambda: [(tables_vmem[2 * k][...], tables_vmem[2 * k + 1][...]) for k in range(4)]
 
     def gradient(c):
         grad_copy(c).wait_recv()
-        moved = state[:, cols(c)] + given[:, cols(c)].astype(F32)
+        moved = state[0, :, cols(c)] + given[:, cols(c)].astype(F32)
         table = tables()
         squeezed = dot3(table[0], halves(moved), (1, 0))
         band = dot3(halves(squeezed), table[2], (1, 0))
         bands[place, band_rows(c), :] = band.T.astype(BF)
         for k in range(replicas - 1):
             band_copy(k, c).start()
-        state[:, cols(c)] = moved - decode_tile(band, table)
-        store(c).start()
+        state[0, :, cols(c)] = moved - decode_tile(band, table)
 
     def shared(c):
         for k in range(replicas - 1):
@@ -353,14 +346,15 @@
             total = total + bands[k, band_rows(c), :].astype(F32)
         tile = decode_tile(total.T, tables()) * (1.0 / replicas)
         update[:, cols(c)] = tile.astype(BF)
-        store_update(c).start()
+        for k in range(replicas - 1):
+            band_copy(k, c).wait_send()
 
     for k in range(3):
         loads[k].wait()
     for t in range(tiles):
         expert(0, rows, gate, up, 0, t)
     first = parts // 2
-    behind = 2
+    behind = 3
     for k in range(first + behind):
         pass_weight(k)
         if k >= behind:
@@ -382,7 +376,8 @@
         token_copy(k).wait_recv()
     expert(rows, rows, gate, up, 0, 0)
     pass_weight(parts - 1)
-    share_weight(parts - behind)
+    share_weight(parts - 3)
+    share_weight(parts - 2)
     expert(rows, rows, gate, up, 0, 1)
     pass_down(0)
     expert(rows, rows, gate_y, up_y, units, 0)
@@ -405,36 +400,6 @@
     own_half(1)
     share_down(2)
 
-    lag = 2
-
-    @pl.loop(0, chunks + lag + 1)
-    def _(c):
-        @pl.when(c < chunks)
-        def _():
-            lend(c)
-
-        @pl.when(c + 4 < chunks)
-        def _():
-            pass_down(c + 4)
-
-        @pl.when(c + 3 < chunks)
-        def _():
-            share_down(c + 3)
-
-        @pl.when(c + 2 < chunks)
-        def _():
-            take_down(c + 2)
-            peer_half(c + 2)
-            own_half(c + 2)
-
-        @pl.when((c >= lag) & (c < chunks + lag))
-        def _():
-            gradient(c - lag)
-
-        @pl.when(c > lag)
-        def _():
-            shared(c - lag - 1)
-
     combine_copy().wait_send()
     for k in range(2):
         token_copy(k).wait_send()
@@ -442,17 +407,43 @@
         for kind in range(2, 6):
             weight_copy(kind, k).wait_send()
 
-    @pl.loop(0, chunks)
+    lag, rest = 1, 2
+
+    @pl.loop(0, chunks + lag + rest)
     def _(c):
-        for kind in range(6, 10):
-            down_copy(kind, c).wait_send()
-        for k in range(2):
-            half_copy(k, c).wait_send()
-        grad_copy(c).wait_send()
-        for k in range(replicas - 1):
-            band_copy(k, c).wait_send()
-        store(c).wait()
-        store_update(c).wait()
+        @pl.when((c >= 2) & (c < chunks + 2))
+        def _():
+            for kind in range(6, 10):
+                down_copy(kind, c - 2).wait_send()
+            for k in range(2):
+                half_copy(k, c - 2).wait_send()
+            grad_copy(c - 2).wait_send()
+
+        @pl.when(c < chunks)
+        def _():
+            lend(c)
+
+        @pl.when(c + 4 < chunks)
+        def _():
+            pass_down(c + 4)
+
+        @pl.when(c + 3 < chunks)
+        def _():
+            share_down(c + 3)
+
+        @pl.when(c + 2 < chunks)
+        def _():
+            take_down(c + 2)
+            peer_half(c + 2)
+            own_half(c + 2)
+
+        @pl.when((c >= lag) & (c < chunks + lag))
+        def _():
+            gradient(c - lag)
+
+        @pl.when(c >= lag + rest)
+        def _():
+            shared(c - lag - rest)
 
 
 def split_step(
@@ -467,27 +458,24 @@
     return pl.pallas_call(
         functools.partial(split_kernel, factor, replicas),
         in_specs=[hbm] * 3 + [pl.BlockSpec(memory_space=pltpu.SMEM)] + [hbm] * 12,
-        out_specs=[hbm, hbm],
-        out_shape=[
-            jax.ShapeDtypeStruct((1, units, width), F32),
-            jax.ShapeDtypeStruct((units, width), BF),
-        ],
+        out_specs=[pl.BlockSpec(memory_space=pltpu.VMEM)] * 2,
+        out_shape=[pltpu.VMEM((1, units, width), F32), block(units, width)],
         scratch_shapes=[
             block(2 * rows, width), block(rows, width), block(rows), block(rows),
             pltpu.VMEM((2, rows, 128), F32),
             block(width, units), block(width, units), block(width, units), block(width, units),
             block(2 * units, width), block(2 * rows, 2 * units), block(2 * units, 2 * rows),
             pltpu.VMEM((2 * rows, width), F32), block(2 * rows, width), block(2 * rows, width),
-            block(units, width), block(units, width), pltpu.VMEM((units, width), F32),
-            block(replicas, width // SPAN * BAND, units // SPAN * BAND), block(units, width),
+            block(units, width), block(units, width),
+            block(replicas, width // SPAN * BAND, units // SPAN * BAND),
         ]
         + [block(*t.shape) for t in tables]
         + [
             pltpu.SemaphoreType.DMA((count,)), pltpu.SemaphoreType.DMA((count,)),
-            pltpu.SemaphoreType.DMA((15 + 2 * chunks,)),
+            pltpu.SemaphoreType.DMA((15,)),
         ],
         compiler_params=pltpu.CompilerParams(
-            collective_id=0, has_side_effects=True, vmem_limit_bytes=60 << 20
+            collective_id=0, has_side_effects=True, vmem_limit_bytes=48 << 20
         ),
         name="split_step",
     )(tokens, target, combine, filled, w_gate, w_up, w_down, momentum, *tables)

time: 122 us -> 116 us (0.951)
  Pallas kernels: 114 us -> 111 us
  local copies, waits for them, and re-layouts: 6.39 us -> 3.59 us
    pallas_call x1, Pallas kernels: 114 us -> 111 us  [split_step(): pl.pallas_call(functools.partial(split_kernel, factor, replicas), in_spec...]
    unnamed x4 -> x2, local copies, waits for them, and re-layouts: 6.39 us -> 3.59 us
where the time goes in v4:
time: 116 us
  Pallas kernels  111 us (96%)
  local copies, waits for them, and re-layouts  3.59 us (3%)
  between operations  1.29 us (1%)
    pallas_call x1, Pallas kernels, split_step(): pl.pallas_call(functools.partial(split_kernel, factor, replicas), in_spec...  111 us
    unnamed x2, local copies, waits for them, and re-layouts  3.59 us

profile of v4, /device:TPU:0, one launch (start us, length us, event | category | flops | bytes accessed | tf_op | source)
XLA Modules:
  0.0 116.2 jit_solution(6176196428962807319)
XLA Ops:
  1.3 111.3 %split_step.1 = (f32[1,512,2304]{2,1,0:T(8,128)S(1)}, bf16[512,2304]{1,0:T(8,128)(2,1)S(1)}) custom-call(bf16[256,2304]{1,0:T(8,128)(2,1)} %tokens_hbm.1, bf16[256,2304]{1,0:T(8,128)(2,1)} %target_hbm.1, bf16[256]{0:T(256)(128)(2,1)} %combine_hbm.1, s32[1]{0:T(128)S(6)} %copy.22.filled, bf16[2304,512]{1,0:T(8,128)(2,1)} %gate_hbm.1, ...), custom_call_target="tpu_custom_call" | custom-call | tf_op jit(solution)/shard_map/split_step/pallas_call | solution.py:458
  112.6 2.2 %copy.20 = f32[1,512,2304]{2,1,0:T(8,128)} copy(f32[1,512,2304]{2,1,0:T(8,128)S(1)} %get-tuple-element.2) | data formatting | bytes 9437184
  114.8 1.4 %copy.21 = bf16[512,2304]{1,0:T(8,128)(2,1)} copy(bf16[512,2304]{1,0:T(8,128)(2,1)S(1)} %get-tuple-element.3) | data formatting | bytes 4718592

commit v5 on v4

--- a/solution.py
+++ b/solution.py
@@ -128,12 +128,12 @@
     return [jnp.asarray(np.ascontiguousarray(p)) for p in pieces]
 
 
-def remote(src, dst, send, recv, index, axis, peer):
+def remote(src, dst, send, recv, axis, peer):
     return pltpu.make_async_remote_copy(
         src_ref=src,
         dst_ref=dst,
-        send_sem=send.at[index],
-        recv_sem=recv.at[index],
+        send_sem=send,
+        recv_sem=recv,
         device_id={axis: peer},
         device_id_type=pl.DeviceIdType.MESH,
     )
@@ -165,24 +165,25 @@
     tiles = units // TILE
     parts = 2 * CUTS * tiles
 
-    sizes = [2, 1] + [parts] * 4 + [chunks] * (7 + replicas - 1)
-    starts = [sum(sizes[:k]) for k in range(len(sizes) + 1)]
-
-    def link(kind, index, src, dst, axis, peer):
-        return remote(src, dst, send, recv, starts[kind] + index, axis, peer)
+    sizes = [1, 1, parts, parts, 2] + [chunks] * 6
+    starts = [sum(sizes[:k]) for k in range(len(sizes))]
+
+    def link(kind, group, index, src, dst, axis, peer):
+        return remote(src, dst, send.at[kind], recv.at[starts[group] + index], axis, peer)
+
+    def sent_all(kind, ref):
+        link(kind, 0, 0, ref, ref, "narrow", x_peer).wait_send()
 
     def cols(c):
         if isinstance(c, int):
             return pl.ds(c * TILE, TILE)
         return pl.ds(pl.multiple_of(c * TILE, TILE), TILE)
 
-    def token_copy(k):
-        part = rows // 2
-        src = tokens_hbm.at[pl.ds(k * part, part)]
-        return link(0, k, src, tok.at[pl.ds(rows + k * part, part)], "narrow", x_peer)
+    def token_copy():
+        return link(0, 0, 0, tokens_hbm, tok.at[pl.ds(rows, rows)], "narrow", x_peer)
 
     def combine_copy():
-        return link(1, 0, combine_hbm, combine_x, "narrow", x_peer)
+        return link(1, 1, 0, combine_hbm, combine_x, "narrow", x_peer)
 
     def piece(k, ref, owner):
         first = pl.multiple_of(owner * deep + k % CUTS * cut, 16)
@@ -191,12 +192,15 @@
     def weight_copy(kind, k):
         mine, theirs = ((gate_hbm, gate_y), (up_hbm, up_y))[k // CUTS % 2]
         if kind == 2:
-            return link(2, k, piece(k, mine, quarter), piece(k, theirs, quarter), "narrow", y_peer)
+            there = piece(k, theirs, quarter)
+            return link(2, 2, k, piece(k, mine, quarter), there, "narrow", y_peer)
         if kind == 5:
             there = piece(k, theirs, (quarter + 2) % 4)
-            return link(5, k, there, there, "wide", twin)
+            return link(5, 4, k // (parts // 2), there, there, "wide", twin)
         here = piece(k, theirs, quarter)
-        return link(kind, k, here, here, "wide", z_peer if kind == 3 else twin)
+        if kind == 3:
+            return link(3, 3, k, here, here, "wide", z_peer)
+        return link(4, 4, k // (parts // 2), here, here, "wide", twin)
 
     def down_piece(c, ref, first, owner):
         return ref.at[pl.ds(pl.multiple_of(first + owner * flat, 16), flat), cols(c)]
@@ -204,19 +208,24 @@
     def down_copy(kind, c):
         if kind == 6:
             src = down_piece(c, down_hbm, 0, quarter)
-            return link(6, c, src, down_piece(c, down, units, quarter), "narrow", y_peer)
+            return link(6, 5, c, src, down_piece(c, down, units, quarter), "narrow", y_peer)
         if kind == 9:
             there = down_piece(c, down, units, (quarter + 2) % 4)
-            return link(9, c, there, there, "wide", twin)
+            return link(9, 7, c, there, there, "wide", twin)
         here = down_piece(c, down, units, quarter)
-        return link(kind, c, here, here, "wide", z_peer if kind == 7 else twin)
+        if kind == 7:
+            return link(7, 6, c, here, here, "wide", z_peer)
+        return link(8, 7, c, here, here, "wide", twin)
 
     def half_copy(k, c):
         src, dst = sent.at[pl.ds(k * rows, rows), cols(c)], came.at[pl.ds(k * rows, rows), cols(c)]
-        return link(10 + k, c, src, dst, "narrow", x_peer)
+        return link(10, 8, c, src, dst, "narrow", x_peer)
+
+    def halves_copy(c):
+        return link(10, 8, c, sent.at[:, cols(c)], came.at[:, cols(c)], "narrow", x_peer)
 
     def grad_copy(c):
-        return link(12, c, lent.at[:, cols(c)], given.at[:, cols(c)], "narrow", y_peer)
+        return link(11, 9, c, lent.at[:, cols(c)], given.at[:, cols(c)], "narrow", y_peer)
 
     kept_t = TILE // SPAN * BAND
 
@@ -225,7 +234,11 @@
 
     def band_copy(k, c):
         mine = bands.at[place, band_rows(c)]
-        return link(13 + k, c, mine, mine, "wide", others[k])
+        return link(12, 10, c, mine, mine, "wide", others[k])
+
+    def bands_copy(c):
+        there = bands.at[pl.ds(0, replicas - 1), band_rows(c)]
+        return link(12, 10, c, there, there, "wide", others[0])
 
     def load(k, src, dst):
         return pltpu.make_async_copy(src, dst, local.at[k])
@@ -249,8 +262,7 @@
         copy.start()
     pl.semaphore_wait(barrier, 1 + replicas)
     combine_copy().start()
-    for k in range(2):
-        token_copy(k).start()
+    token_copy().start()
     for k in range(parts):
         weight_copy(2, k).start()
 
@@ -276,10 +288,10 @@
         weight_copy(3, k).wait_recv()
         weight_copy(5, k).start()
 
-    def take_weights(first, last):
-        for k in range(first, last):
-            weight_copy(4, k).wait_recv()
-            weight_copy(5, k).wait_recv()
+    all_pieces = gate_y.at[pl.ds(0, 2 * deep)]
+
+    def take_weights(k):
+        link(4, 4, k, all_pieces, all_pieces, "wide", twin).wait_recv()
 
     def pass_down(c):
         down_copy(6, c).wait_recv()
@@ -291,8 +303,8 @@
         down_copy(9, c).start()
 
     def take_down(c):
-        down_copy(8, c).wait_recv()
-        down_copy(9, c).wait_recv()
+        both = down.at[pl.ds(units, 2 * flat), cols(c)]
+        link(8, 7, c, both, both, "wide", twin).wait_recv()
 
     def wide_weight(k):
         return jnp.concatenate([weight[k]] * (TILE // weight.shape[2]), axis=1)
@@ -313,10 +325,9 @@
         kept[:rows, cols(c)] = value
 
     def lend(c):
-        half_copy(1, c).wait_recv()
+        halves_copy(c).wait_recv()
         scale = wide_weight(0)
         mine = kept[:rows, cols(c)] + scale * (scale * came[rows:, cols(c)].astype(F32))
-        half_copy(0, c).wait_recv()
         theirs = kept[rows:, cols(c)] + came[:rows, cols(c)].astype(F32)
         error = jnp.concatenate([mine.astype(BF), theirs.astype(BF)], axis=0)
         grad = jnp.dot(hidden_t[units:, :], error, preferred_element_type=F32)
@@ -339,15 +350,12 @@
         state[0, :, cols(c)] = moved - decode_tile(band, table)
 
     def shared(c):
-        for k in range(replicas - 1):
-            band_copy(k, c).wait_recv()
+        bands_copy(c).wait_recv()
         total = bands[0, band_rows(c), :].astype(F32)
         for k in range(1, replicas):
             total = total + bands[k, band_rows(c), :].astype(F32)
         tile = decode_tile(total.T, tables()) * (1.0 / replicas)
         update[:, cols(c)] = tile.astype(BF)
-        for k in range(replicas - 1):
-            band_copy(k, c).wait_send()
 
     for k in range(3):
         loads[k].wait()
@@ -359,7 +367,7 @@
         pass_weight(k)
         if k >= behind:
             share_weight(k - behind)
-    take_weights(0, first)
+    take_weights(0)
     expert(0, rows, gate_y, up_y, units, 0)
     for k in range(first + behind, parts - 1):
         share_weight(k - behind)
@@ -372,18 +380,17 @@
         value = ref[...].astype(F32).reshape(1, rows)
         live = jnp.where(row_ids < filled[0], value, 0.0)
         weight[k] = jnp.broadcast_to(live, (weight.shape[2], rows)).T
-    for k in range(2):
-        token_copy(k).wait_recv()
+    token_copy().wait_recv()
     expert(rows, rows, gate, up, 0, 0)
     pass_weight(parts - 1)
     share_weight(parts - 3)
     share_weight(parts - 2)
+    pass_down(0)
     expert(rows, rows, gate, up, 0, 1)
-    pass_down(0)
+    pass_down(1)
+    share_weight(parts - 1)
     expert(rows, rows, gate_y, up_y, units, 0)
-    share_weight(parts - 1)
-    pass_down(1)
-    take_weights(first, parts)
+    take_weights(1)
     expert(rows, rows, gate_y, up_y, units, 1)
     for copy in loads[4:]:
         copy.wait()
@@ -401,24 +408,14 @@
     share_down(2)
 
     combine_copy().wait_send()
-    for k in range(2):
-        token_copy(k).wait_send()
-    for k in range(parts):
-        for kind in range(2, 6):
-            weight_copy(kind, k).wait_send()
+    token_copy().wait_send()
+    for kind in range(2, 6):
+        sent_all(kind, all_pieces)
 
     lag, rest = 1, 2
 
     @pl.loop(0, chunks + lag + rest)
     def _(c):
-        @pl.when((c >= 2) & (c < chunks + 2))
-        def _():
-            for kind in range(6, 10):
-                down_copy(kind, c - 2).wait_send()
-            for k in range(2):
-                half_copy(k, c - 2).wait_send()
-            grad_copy(c - 2).wait_send()
-
         @pl.when(c < chunks)
         def _():
             lend(c)
@@ -444,6 +441,12 @@
         @pl.when(c >= lag + rest)
         def _():
             shared(c - lag - rest)
+
+    for kind in range(6, 10):
+        sent_all(kind, down.at[pl.ds(0, flat)])
+    sent_all(10, sent)
+    sent_all(11, lent)
+    sent_all(12, bands.at[pl.ds(0, replicas - 1)])
 
 
 def split_step(
@@ -454,7 +457,7 @@
     hbm = pl.BlockSpec(memory_space=pl.ANY)
     block = lambda *shape: pltpu.VMEM(shape, BF)
     chunks = width // TILE
-    count = 3 + 8 * CUTS * (units // TILE) + (6 + replicas) * chunks
+    count = 4 + 4 * CUTS * (units // TILE) + 6 * chunks
     return pl.pallas_call(
         functools.partial(split_kernel, factor, replicas),
         in_specs=[hbm] * 3 + [pl.BlockSpec(memory_space=pltpu.SMEM)] + [hbm] * 12,
@@ -471,7 +474,7 @@
         ]
         + [block(*t.shape) for t in tables]
         + [
-            pltpu.SemaphoreType.DMA((count,)), pltpu.SemaphoreType.DMA((count,)),
+            pltpu.SemaphoreType.DMA((13,)), pltpu.SemaphoreType.DMA((count,)),
             pltpu.SemaphoreType.DMA((15,)),
         ],
         compiler_params=pltpu.CompilerParams(

time: 116 us -> 113 us (0.974)
  Pallas kernels: 111 us -> 108 us
    pallas_call x1, Pallas kernels: 111 us -> 108 us  [split_step(): pl.pallas_call(functools.partial(split_kernel, factor, replicas), in_spec...]
where the time goes in v5:
time: 113 us
  Pallas kernels  108 us (96%)
  local copies, waits for them, and re-layouts  3.59 us (3%)
  between operations  1.29 us (1%)
    pallas_call x1, Pallas kernels, split_step(): pl.pallas_call(functools.partial(split_kernel, factor, replicas), in_spec...  108 us
    unnamed x2, local copies, waits for them, and re-layouts  3.59 us

profile of v5, /device:TPU:0, one launch (start us, length us, event | category | flops | bytes accessed | tf_op | source)
XLA Modules:
  0.0 113.0 jit_solution(9323917659055942084)
XLA Ops:
  1.3 108.1 %split_step.1 = (f32[1,512,2304]{2,1,0:T(8,128)S(1)}, bf16[512,2304]{1,0:T(8,128)(2,1)S(1)}) custom-call(bf16[256,2304]{1,0:T(8,128)(2,1)} %tokens_hbm.1, bf16[256,2304]{1,0:T(8,128)(2,1)} %target_hbm.1, bf16[256]{0:T(256)(128)(2,1)} %combine_hbm.1, s32[1]{0:T(128)S(6)} %copy.22.filled, bf16[2304,512]{1,0:T(8,128)(2,1)} %gate_hbm.1, ...), custom_call_target="tpu_custom_call" | custom-call | tf_op jit(solution)/shard_map/split_step/pallas_call | solution.py:461
  109.4 2.2 %copy.20 = f32[1,512,2304]{2,1,0:T(8,128)} copy(f32[1,512,2304]{2,1,0:T(8,128)S(1)} %get-tuple-element.2) | data formatting | bytes 9437184
  111.6 1.4 %copy.21 = bf16[512,2304]{1,0:T(8,128)(2,1)} copy(bf16[512,2304]{1,0:T(8,128)(2,1)S(1)} %get-tuple-element.3) | data formatting | bytes 4718592

commit v6 on v5

--- a/solution.py
+++ b/solution.py
@@ -165,7 +165,8 @@
     tiles = units // TILE
     parts = 2 * CUTS * tiles
 
-    sizes = [1, 1, parts, parts, 2] + [chunks] * 6
+    slim = TILE // 2
+    sizes = [1, 1, parts, parts, 2] + [chunks] * 3 + [2 * chunks] + [chunks] * 2
     starts = [sum(sizes[:k]) for k in range(len(sizes))]
 
     def link(kind, group, index, src, dst, axis, peer):
@@ -217,12 +218,23 @@
             return link(7, 6, c, here, here, "wide", z_peer)
         return link(8, 7, c, here, here, "wide", twin)
 
+    def slim_cols(c):
+        if isinstance(c, int):
+            return pl.ds(c * slim, slim)
+        return pl.ds(pl.multiple_of(c * slim, slim), slim)
+
     def half_copy(k, c):
-        src, dst = sent.at[pl.ds(k * rows, rows), cols(c)], came.at[pl.ds(k * rows, rows), cols(c)]
+        part = pl.ds(k * rows, rows)
+        src, dst = sent.at[part, slim_cols(c)], came.at[part, slim_cols(c)]
         return link(10, 8, c, src, dst, "narrow", x_peer)
 
     def halves_copy(c):
-        return link(10, 8, c, sent.at[:, cols(c)], came.at[:, cols(c)], "narrow", x_peer)
+        at = slim_cols(c)
+        return link(10, 8, c, sent.at[:, at], came.at[:, at], "narrow", x_peer)
+
+    def slim_grad_copy(c):
+        at = slim_cols(c)
+        return link(11, 9, c // 2, lent.at[:, at], given.at[:, at], "narrow", y_peer)
 
     def grad_copy(c):
         return link(11, 9, c, lent.at[:, cols(c)], given.at[:, cols(c)], "narrow", y_peer)
@@ -312,7 +324,7 @@
     def peer_half(c):
         part = jnp.dot(hidden[rows:, :], down[:, cols(c)], preferred_element_type=F32)
         sent[rows:, cols(c)] = part.astype(BF)
-        half_copy(1, c).start()
+        half_copy(1, 2 * c).start()
         scale = wide_weight(1)
         kept[rows:, cols(c)] = scale * (scale * part)
 
@@ -321,20 +333,23 @@
         scale = wide_weight(0)
         value = scale * (scale * part - target[:, cols(c)].astype(F32))
         sent[:rows, cols(c)] = value.astype(BF)
-        half_copy(0, c).start()
+        half_copy(0, 2 * c).start()
+        half_copy(1, 2 * c + 1).start()
+        half_copy(0, 2 * c + 1).start()
         kept[:rows, cols(c)] = value
 
     def lend(c):
+        at = slim_cols(c)
         halves_copy(c).wait_recv()
-        scale = wide_weight(0)
-        mine = kept[:rows, cols(c)] + scale * (scale * came[rows:, cols(c)].astype(F32))
-        theirs = kept[rows:, cols(c)] + came[:rows, cols(c)].astype(F32)
+        scale = weight[0]
+        mine = kept[:rows, at] + scale * (scale * came[rows:, at].astype(F32))
+        theirs = kept[rows:, at] + came[:rows, at].astype(F32)
         error = jnp.concatenate([mine.astype(BF), theirs.astype(BF)], axis=0)
         grad = jnp.dot(hidden_t[units:, :], error, preferred_element_type=F32)
-        lent[:, cols(c)] = (factor * grad).astype(BF)
-        grad_copy(c).start()
+        lent[:, at] = (factor * grad).astype(BF)
+        slim_grad_copy(c).start()
         grad = jnp.dot(hidden_t[:units, :], error, preferred_element_type=F32)
-        state[0, :, cols(c)] = 0.999 * state[0, :, cols(c)] + factor * grad
+        state[0, :, at] = 0.999 * state[0, :, at] + factor * grad
 
     tables = lambda: [(tables_vmem[2 * k][...], tables_vmem[2 * k + 1][...]) for k in range(4)]
 
@@ -418,7 +433,7 @@
     def _(c):
         @pl.when(c < chunks)
         def _():
-            lend(c)
+            lend(2 * c)
 
         @pl.when(c + 4 < chunks)
         def _():
@@ -433,6 +448,10 @@
             take_down(c + 2)
             peer_half(c + 2)
             own_half(c + 2)
+
+        @pl.when(c < chunks)
+        def _():
+            lend(2 * c + 1)
 
         @pl.when((c >= lag) & (c < chunks + lag))
         def _():
@@ -447,6 +466,31 @@
     sent_all(10, sent)
     sent_all(11, lent)
     sent_all(12, bands.at[pl.ds(0, replicas - 1)])
+
+
+def store_kernel(state, update, state_hbm, update_hbm, local):
+    half = update.shape[0] // 2
+    copies = [pltpu.make_async_copy(update, update_hbm, local.at[2])]
+    for k in range(2):
+        part = pl.ds(k * half, half)
+        copies += [pltpu.make_async_copy(state.at[0, part], state_hbm.at[0, part], local.at[k])]
+    for copy in copies:
+        copy.start()
+    for copy in copies:
+        copy.wait()
+
+
+def store_step(state, update):
+    vmem, hbm = pl.BlockSpec(memory_space=pltpu.VMEM), pl.BlockSpec(memory_space=pl.ANY)
+    return pl.pallas_call(
+        store_kernel,
+        in_specs=[vmem] * 2,
+        out_specs=[hbm] * 2,
+        out_shape=[jax.ShapeDtypeStruct(a.shape, a.dtype) for a in (state, update)],
+        scratch_shapes=[pltpu.SemaphoreType.DMA((3,))],
+        compiler_params=pltpu.CompilerParams(vmem_limit_bytes=4 << 20),
+        name="store_step",
+    )(state, update)
 
 
 def split_step(
@@ -457,7 +501,7 @@
     hbm = pl.BlockSpec(memory_space=pl.ANY)
     block = lambda *shape: pltpu.VMEM(shape, BF)
     chunks = width // TILE
-    count = 4 + 4 * CUTS * (units // TILE) + 6 * chunks
+    count = 4 + 4 * CUTS * (units // TILE) + 7 * chunks
     return pl.pallas_call(
         functools.partial(split_kernel, factor, replicas),
         in_specs=[hbm] * 3 + [pl.BlockSpec(memory_space=pltpu.SMEM)] + [hbm] * 12,
@@ -512,10 +556,11 @@
     factor = 1.0 / math.sqrt(total_rows)
     fits = units == 2 * TILE and width % (64 * CUTS) == 0 and tokens.shape[0] % 128 == 0
     if narrow == 4 and replicas % 4 == 0 and fits:
-        return split_step(
+        state, update = split_step(
             tokens, target, combine, filled, w_gate, w_up, w_down, momentum, tables, factor,
             replicas,
         )
+        return store_step(state, update)
     hidden_t, errors = forward(tokens, target, combine, filled, w_gate, w_up, w_down)
     residue, band = grad_step(hidden_t, errors, momentum, tables, factor)
     bands = lax.all_gather(band.astype(BF)[None], "wide", axis=0, tiled=True)

time: 113 us -> 110 us (0.973)
  local copies, waits for them, and re-layouts: 3.59 us -> 0 us
    unnamed x2 -> x0, local copies, waits for them, and re-layouts: 3.59 us -> none
    pallas_call x0 -> x1, Pallas kernels: none -> 2.99 us  [store_step(): pl.pallas_call(store_kernel, in_specs=[vmem] * 2, out_specs=[hbm] * 2, ou...]
    pallas_call x1, Pallas kernels: 108 us -> 105 us  [split_step(): pl.pallas_call(functools.partial(split_kernel, factor, replicas), in_spec...]
where the time goes in v6:
time: 110 us
  Pallas kernels  108 us (98%)
  between operations  1.29 us (1%)
    pallas_call x1, Pallas kernels, split_step(): pl.pallas_call(functools.partial(split_kernel, factor, replicas), in_spec...  105 us
    pallas_call x1, Pallas kernels, store_step(): pl.pallas_call(store_kernel, in_specs=[vmem] * 2, out_specs=[hbm] * 2, ou...  2.99 us

profile of v6, /device:TPU:0, one launch (start us, length us, event | category | flops | bytes accessed | tf_op | source)
XLA Modules:
  0.0 109.7 jit_solution(8263854409732194965)
XLA Ops:
  1.3 105.4 %split_step.1 = (f32[1,512,2304]{2,1,0:T(8,128)S(1)}, bf16[512,2304]{1,0:T(8,128)(2,1)S(1)}) custom-call(bf16[256,2304]{1,0:T(8,128)(2,1)} %tokens_hbm.1, bf16[256,2304]{1,0:T(8,128)(2,1)} %target_hbm.1, bf16[256]{0:T(256)(128)(2,1)} %combine_hbm.1, s32[1]{0:T(128)S(6)} %copy.18.filled, bf16[2304,512]{1,0:T(8,128)(2,1)} %gate_hbm.1, ...), custom_call_target="tpu_custom_call" | custom-call | tf_op jit(solution)/shard_map/split_step/pallas_call | solution.py:505
  106.7 3.0 %store_step.1 = (f32[1,512,2304]{2,1,0:T(8,128)}, bf16[512,2304]{1,0:T(8,128)(2,1)}) custom-call(f32[1,512,2304]{2,1,0:T(8,128)S(1)} %get-tuple-element.4.state, bf16[512,2304]{1,0:T(8,128)(2,1)S(1)} %get-tuple-element.5.update), custom_call_target="tpu_custom_call" | custom-call | tf_op jit(solution)/shard_map/store_step/pallas_call | solution.py:485

commit v7 on v6

--- a/solution.py
+++ b/solution.py
@@ -387,7 +387,6 @@
     for k in range(first + behind, parts - 1):
         share_weight(k - behind)
         pass_weight(k)
-    share_weight(parts - 1 - behind)
     loads[3].wait()
     combine_copy().wait_recv()
     for k, (owner, ref) in enumerate(((me, combine), (x_peer, combine_x))):
@@ -395,22 +394,23 @@
         value = ref[...].astype(F32).reshape(1, rows)
         live = jnp.where(row_ids < filled[0], value, 0.0)
         weight[k] = jnp.broadcast_to(live, (weight.shape[2], rows)).T
+    share_weight(parts - 1 - behind)
+    pass_weight(parts - 1)
     token_copy().wait_recv()
     expert(rows, rows, gate, up, 0, 0)
-    pass_weight(parts - 1)
     share_weight(parts - 3)
-    share_weight(parts - 2)
     pass_down(0)
     expert(rows, rows, gate, up, 0, 1)
+    share_weight(parts - 2)
     pass_down(1)
+    expert(rows, rows, gate_y, up_y, units, 0)
     share_weight(parts - 1)
-    expert(rows, rows, gate_y, up_y, units, 0)
+    pass_down(2)
+    share_down(0)
     take_weights(1)
     expert(rows, rows, gate_y, up_y, units, 1)
     for copy in loads[4:]:
         copy.wait()
-    pass_down(2)
-    share_down(0)
     take_down(0)
     peer_half(0)
     expert(0, rows, gate_y, up_y, units, 1)

time: 110 us -> 109 us (level)
  no operation moved by 1% of the time
where the time goes in v7:
time: 109 us
  Pallas kernels  107 us (98%)
  between operations  1.29 us (1%)
    pallas_call x1, Pallas kernels, split_step(): pl.pallas_call(functools.partial(split_kernel, factor, replicas), in_spec...  104 us
    pallas_call x1, Pallas kernels, store_step(): pl.pallas_call(store_kernel, in_specs=[vmem] * 2, out_specs=[hbm] * 2, ou...  2.99 us

profile of v7, /device:TPU:0, one launch (start us, length us, event | category | flops | bytes accessed | tf_op | source)
XLA Modules:
  0.0 108.7 jit_solution(11763805682867230202)
XLA Ops:
  1.3 104.4 %split_step.1 = (f32[1,512,2304]{2,1,0:T(8,128)S(1)}, bf16[512,2304]{1,0:T(8,128)(2,1)S(1)}) custom-call(bf16[256,2304]{1,0:T(8,128)(2,1)} %tokens_hbm.1, bf16[256,2304]{1,0:T(8,128)(2,1)} %target_hbm.1, bf16[256]{0:T(256)(128)(2,1)} %combine_hbm.1, s32[1]{0:T(128)S(6)} %copy.18.filled, bf16[2304,512]{1,0:T(8,128)(2,1)} %gate_hbm.1, ...), custom_call_target="tpu_custom_call" | custom-call | tf_op jit(solution)/shard_map/split_step/pallas_call | solution.py:505
  105.7 3.0 %store_step.1 = (f32[1,512,2304]{2,1,0:T(8,128)}, bf16[512,2304]{1,0:T(8,128)(2,1)}) custom-call(f32[1,512,2304]{2,1,0:T(8,128)S(1)} %get-tuple-element.4.state, bf16[512,2304]{1,0:T(8,128)(2,1)S(1)} %get-tuple-element.5.update), custom_call_target="tpu_custom_call" | custom-call | tf_op jit(solution)/shard_map/store_step/pallas_call | solution.py:485

commit v8 on v7

--- a/solution.py
+++ b/solution.py
@@ -146,10 +146,10 @@
     tables_hbm, (state, update) = refs[:8], refs[8:10]
     (
         tok, target, combine, combine_x, weight, gate, up, gate_y, up_y, down, hidden, hidden_t,
-        kept, sent, came, lent, given, bands,
-    ) = refs[10:28]
-    tables_vmem = refs[28:36]
-    send, recv, local = refs[36:39]
+        kept, sent, came, lent, given, bands, early, early_x, own_band,
+    ) = refs[10:31]
+    tables_vmem = refs[31:39]
+    send, recv, local = refs[39:42]
     me, place = lax.axis_index("narrow"), lax.axis_index("wide")
     x_peer = me + 1 - 2 * (me % 2)
     y_peer = (me + 2) % 4
@@ -166,7 +166,7 @@
     parts = 2 * CUTS * tiles
 
     slim = TILE // 2
-    sizes = [1, 1, parts, parts, 2] + [chunks] * 3 + [2 * chunks] + [chunks] * 2
+    sizes = [1, 1, parts, parts, 2] + [chunks] * 3 + [2 * chunks] + [chunks] * 2 + [1]
     starts = [sum(sizes[:k]) for k in range(len(sizes))]
 
     def link(kind, group, index, src, dst, axis, peer):
@@ -251,6 +251,9 @@
     def bands_copy(c):
         there = bands.at[pl.ds(0, replicas - 1), band_rows(c)]
         return link(12, 10, c, there, there, "wide", others[0])
+
+    def early_copy():
+        return link(13, 11, 0, early, early_x, "narrow", y_peer)
 
     def load(k, src, dst):
         return pltpu.make_async_copy(src, dst, local.at[k])
@@ -338,6 +341,15 @@
         half_copy(0, 2 * c + 1).start()
         kept[:rows, cols(c)] = value
 
+    tables = lambda: [(tables_vmem[2 * k][...], tables_vmem[2 * k + 1][...]) for k in range(4)]
+
+    def encode(value):
+        table = tables()
+        squeezed = dot3(table[0], halves(value), (1, 0))
+        return dot3(halves(squeezed), table[2], (1, 0))
+
+    last = chunks - 1
+
     def lend(c):
         at = slim_cols(c)
         halves_copy(c).wait_recv()
@@ -347,22 +359,35 @@
         error = jnp.concatenate([mine.astype(BF), theirs.astype(BF)], axis=0)
         grad = jnp.dot(hidden_t[units:, :], error, preferred_element_type=F32)
         lent[:, at] = (factor * grad).astype(BF)
+
+        @pl.when(c == 2 * last + 1)
+        def _():
+            early[...] = encode(lent[:, cols(last)].astype(F32)).T.astype(BF)
+            early_copy().start()
+
         slim_grad_copy(c).start()
         grad = jnp.dot(hidden_t[:units, :], error, preferred_element_type=F32)
         state[0, :, at] = 0.999 * state[0, :, at] + factor * grad
 
-    tables = lambda: [(tables_vmem[2 * k][...], tables_vmem[2 * k + 1][...]) for k in range(4)]
+        @pl.when(c == 2 * last + 1)
+        def _():
+            own_band[...] = encode(state[0, :, cols(last)]).T
+
+    def send_band(c, value):
+        bands[place, band_rows(c), :] = value.astype(BF)
+        for k in range(replicas - 1):
+            band_copy(k, c).start()
 
     def gradient(c):
         grad_copy(c).wait_recv()
         moved = state[0, :, cols(c)] + given[:, cols(c)].astype(F32)
-        table = tables()
-        squeezed = dot3(table[0], halves(moved), (1, 0))
-        band = dot3(halves(squeezed), table[2], (1, 0))
-        bands[place, band_rows(c), :] = band.T.astype(BF)
-        for k in range(replicas - 1):
-            band_copy(k, c).start()
-        state[0, :, cols(c)] = moved - decode_tile(band, table)
+        band = encode(moved)
+
+        @pl.when(c != last)
+        def _():
+            send_band(c, band.T)
+
+        state[0, :, cols(c)] = moved - decode_tile(band, tables())
 
     def shared(c):
         bands_copy(c).wait_recv()
@@ -427,7 +452,7 @@
     for kind in range(2, 6):
         sent_all(kind, all_pieces)
 
-    lag, rest = 1, 2
+    lag, rest = 1, 1
 
     @pl.loop(0, chunks + lag + rest)
     def _(c):
@@ -449,13 +474,22 @@
             peer_half(c + 2)
             own_half(c + 2)
 
+        @pl.when(c == last)
+        def _():
+            gradient(c - lag)
+
         @pl.when(c < chunks)
         def _():
             lend(2 * c + 1)
 
-        @pl.when((c >= lag) & (c < chunks + lag))
+        @pl.when((c >= lag) & (c < chunks + lag) & (c != last))
         def _():
             gradient(c - lag)
+
+        @pl.when(c == last)
+        def _():
+            early_copy().wait_recv()
+            send_band(last, own_band[...] + early_x[...].astype(F32))
 
         @pl.when(c >= lag + rest)
         def _():
@@ -463,6 +497,7 @@
 
     for kind in range(6, 10):
         sent_all(kind, down.at[pl.ds(0, flat)])
+    early_copy().wait_send()
     sent_all(10, sent)
     sent_all(11, lent)
     sent_all(12, bands.at[pl.ds(0, replicas - 1)])
@@ -501,7 +536,8 @@
     hbm = pl.BlockSpec(memory_space=pl.ANY)
     block = lambda *shape: pltpu.VMEM(shape, BF)
     chunks = width // TILE
-    count = 4 + 4 * CUTS * (units // TILE) + 7 * chunks
+    count = 5 + 4 * CUTS * (units // TILE) + 7 * chunks
+    band_shape = (TILE // SPAN * BAND, units // SPAN * BAND)
     return pl.pallas_call(
         functools.partial(split_kernel, factor, replicas),
         in_specs=[hbm] * 3 + [pl.BlockSpec(memory_space=pltpu.SMEM)] + [hbm] * 12,
@@ -515,10 +551,11 @@
             pltpu.VMEM((2 * rows, width), F32), block(2 * rows, width), block(2 * rows, width),
             block(units, width), block(units, width),
             block(replicas, width // SPAN * BAND, units // SPAN * BAND),
+            block(*band_shape), block(*band_shape), pltpu.VMEM(band_shape, F32),
         ]
         + [block(*t.shape) for t in tables]
         + [
-            pltpu.SemaphoreType.DMA((13,)), pltpu.SemaphoreType.DMA((count,)),
+            pltpu.SemaphoreType.DMA((14,)), pltpu.SemaphoreType.DMA((count,)),
             pltpu.SemaphoreType.DMA((15,)),
         ],
         compiler_params=pltpu.CompilerParams(

time: 109 us -> 107 us (0.982)
    pallas_call x1, Pallas kernels: 104 us -> 103 us  [split_step(): pl.pallas_call(functools.partial(split_kernel, factor, replicas), in_spec...]
where the time goes in v8:
time: 107 us
  Pallas kernels  106 us (99%)
  between operations  1.29 us (1%)
    pallas_call x1, Pallas kernels, split_step(): pl.pallas_call(functools.partial(split_kernel, factor, replicas), in_spec...  103 us
    pallas_call x1, Pallas kernels, store_step(): pl.pallas_call(store_kernel, in_specs=[vmem] * 2, out_specs=[hbm] * 2, ou...  2.99 us

profile of v8, /device:TPU:0, one launch (start us, length us, event | category | flops | bytes accessed | tf_op | source)
XLA Modules:
  0.0 107.0 jit_solution(1697676524972036194)
XLA Ops:
  1.3 102.8 %split_step.1 = (f32[1,512,2304]{2,1,0:T(8,128)S(1)}, bf16[512,2304]{1,0:T(8,128)(2,1)S(1)}) custom-call(bf16[256,2304]{1,0:T(8,128)(2,1)} %tokens_hbm.1, bf16[256,2304]{1,0:T(8,128)(2,1)} %target_hbm.1, bf16[256]{0:T(256)(128)(2,1)} %combine_hbm.1, s32[1]{0:T(128)S(6)} %copy.18.filled, bf16[2304,512]{1,0:T(8,128)(2,1)} %gate_hbm.1, ...), custom_call_target="tpu_custom_call" | custom-call | tf_op jit(solution)/shard_map/split_step/pallas_call | solution.py:541
  104.1 3.0 %store_step.1 = (f32[1,512,2304]{2,1,0:T(8,128)}, bf16[512,2304]{1,0:T(8,128)(2,1)}) custom-call(f32[1,512,2304]{2,1,0:T(8,128)S(1)} %get-tuple-element.4.state, bf16[512,2304]{1,0:T(8,128)(2,1)S(1)} %get-tuple-element.5.update), custom_call_target="tpu_custom_call" | custom-call | tf_op jit(solution)/shard_map/store_step/pallas_call | solution.py:520

commit v9 on v8

--- a/solution.py
+++ b/solution.py
@@ -166,7 +166,7 @@
     parts = 2 * CUTS * tiles
 
     slim = TILE // 2
-    sizes = [1, 1, parts, parts, 2] + [chunks] * 3 + [2 * chunks] + [chunks] * 2 + [1]
+    sizes = [1, 1, parts, parts, 2] + [chunks] * 3 + [2 * chunks] + [chunks] * 2 + [2]
     starts = [sum(sizes[:k]) for k in range(len(sizes))]
 
     def link(kind, group, index, src, dst, axis, peer):
@@ -252,8 +252,8 @@
         there = bands.at[pl.ds(0, replicas - 1), band_rows(c)]
         return link(12, 10, c, there, there, "wide", others[0])
 
-    def early_copy():
-        return link(13, 11, 0, early, early_x, "narrow", y_peer)
+    def early_copy(h):
+        return link(13, 11, h, early.at[h], early_x.at[h], "narrow", y_peer)
 
     def load(k, src, dst):
         return pltpu.make_async_copy(src, dst, local.at[k])
@@ -345,8 +345,10 @@
 
     def encode(value):
         table = tables()
+        width = value.shape[1]
+        right = tuple(part[:width, : width // SPAN * BAND] for part in table[2])
         squeezed = dot3(table[0], halves(value), (1, 0))
-        return dot3(halves(squeezed), table[2], (1, 0))
+        return dot3(halves(squeezed), right, (1, 0))
 
     last = chunks - 1
 
@@ -360,23 +362,36 @@
         grad = jnp.dot(hidden_t[units:, :], error, preferred_element_type=F32)
         lent[:, at] = (factor * grad).astype(BF)
 
-        @pl.when(c == 2 * last + 1)
-        def _():
-            early[...] = encode(lent[:, cols(last)].astype(F32)).T.astype(BF)
-            early_copy().start()
+        for h in range(2):
+
+            @pl.when(c == 2 * last + h)
+            def _():
+                part = lent[:, slim_cols(2 * last + h)].astype(F32)
+                early[h] = encode(part).T.astype(BF)
+                early_copy(h).start()
 
         slim_grad_copy(c).start()
         grad = jnp.dot(hidden_t[:units, :], error, preferred_element_type=F32)
         state[0, :, at] = 0.999 * state[0, :, at] + factor * grad
 
-        @pl.when(c == 2 * last + 1)
-        def _():
-            own_band[...] = encode(state[0, :, cols(last)]).T
+        for h in range(2):
+
+            @pl.when(c == 2 * last + h)
+            def _():
+                own_band[h] = encode(state[0, :, slim_cols(2 * last + h)]).T
 
     def send_band(c, value):
         bands[place, band_rows(c), :] = value.astype(BF)
         for k in range(replicas - 1):
             band_copy(k, c).start()
+
+    def send_last(h):
+        early_copy(h).wait_recv()
+        at = pl.ds(last * kept_t + h * (kept_t // 2), kept_t // 2)
+        bands[place, at, :] = (own_band[h] + early_x[h].astype(F32)).astype(BF)
+        mine = bands.at[place, at]
+        for k in range(replicas - 1):
+            link(12, 10, last, mine, mine, "wide", others[k]).start()
 
     def gradient(c):
         grad_copy(c).wait_recv()
@@ -482,22 +497,26 @@
         def _():
             lend(2 * c + 1)
 
+        @pl.when(c == chunks)
+        def _():
+            shared(c - lag - rest)
+
         @pl.when((c >= lag) & (c < chunks + lag) & (c != last))
         def _():
             gradient(c - lag)
 
         @pl.when(c == last)
         def _():
-            early_copy().wait_recv()
-            send_band(last, own_band[...] + early_x[...].astype(F32))
-
-        @pl.when(c >= lag + rest)
+            send_last(0)
+            send_last(1)
+
+        @pl.when((c >= lag + rest) & (c != chunks))
         def _():
             shared(c - lag - rest)
 
     for kind in range(6, 10):
         sent_all(kind, down.at[pl.ds(0, flat)])
-    early_copy().wait_send()
+    sent_all(13, early)
     sent_all(10, sent)
     sent_all(11, lent)
     sent_all(12, bands.at[pl.ds(0, replicas - 1)])
@@ -536,8 +555,8 @@
     hbm = pl.BlockSpec(memory_space=pl.ANY)
     block = lambda *shape: pltpu.VMEM(shape, BF)
     chunks = width // TILE
-    count = 5 + 4 * CUTS * (units // TILE) + 7 * chunks
-    band_shape = (TILE // SPAN * BAND, units // SPAN * BAND)
+    count = 6 + 4 * CUTS * (units // TILE) + 7 * chunks
+    band_shape = (2, TILE // 2 // SPAN * BAND, units // SPAN * BAND)
     return pl.pallas_call(
         functools.partial(split_kernel, factor, replicas),
         in_specs=[hbm] * 3 + [pl.BlockSpec(memory_space=pltpu.SMEM)] + [hbm] * 12,

time: 107 us -> 107 us (level)
  no operation moved by 1% of the time
where the time goes in v9:
time: 107 us
  Pallas kernels  105 us (98%)
  between operations  1.29 us (1%)
    pallas_call x1, Pallas kernels, split_step(): pl.pallas_call(functools.partial(split_kernel, factor, replicas), in_spec...  102 us
    pallas_call x1, Pallas kernels, store_step(): pl.pallas_call(store_kernel, in_specs=[vmem] * 2, out_specs=[hbm] * 2, ou...  2.99 us

profile of v9, /device:TPU:0, one launch (start us, length us, event | category | flops | bytes accessed | tf_op | source)
XLA Modules:
  0.0 106.6 jit_solution(13610034323971404437)
XLA Ops:
  1.3 102.3 %split_step.1 = (f32[1,512,2304]{2,1,0:T(8,128)S(1)}, bf16[512,2304]{1,0:T(8,128)(2,1)S(1)}) custom-call(bf16[256,2304]{1,0:T(8,128)(2,1)} %tokens_hbm.1, bf16[256,2304]{1,0:T(8,128)(2,1)} %target_hbm.1, bf16[256]{0:T(256)(128)(2,1)} %combine_hbm.1, s32[1]{0:T(128)S(6)} %copy.18.filled, bf16[2304,512]{1,0:T(8,128)(2,1)} %gate_hbm.1, ...), custom_call_target="tpu_custom_call" | custom-call | tf_op jit(solution)/shard_map/split_step/pallas_call | solution.py:560
  103.6 3.0 %store_step.1 = (f32[1,512,2304]{2,1,0:T(8,128)}, bf16[512,2304]{1,0:T(8,128)(2,1)}) custom-call(f32[1,512,2304]{2,1,0:T(8,128)S(1)} %get-tuple-element.4.state, bf16[512,2304]{1,0:T(8,128)(2,1)S(1)} %get-tuple-element.5.update), custom_call_target="tpu_custom_call" | custom-call | tf_op jit(solution)/shard_map/store_step/pallas_call | solution.py:539

commit v10 on v9

--- a/solution.py
+++ b/solution.py
@@ -427,7 +427,8 @@
     for k in range(first + behind, parts - 1):
         share_weight(k - behind)
         pass_weight(k)
-    loads[3].wait()
+    for copy in loads[3:]:
+        copy.wait()
     combine_copy().wait_recv()
     for k, (owner, ref) in enumerate(((me, combine), (x_peer, combine_x))):
         row_ids = owner * rows + lax.broadcasted_iota(jnp.int32, (1, rows), 1)
@@ -449,8 +450,6 @@
     share_down(0)
     take_weights(1)
     expert(rows, rows, gate_y, up_y, units, 1)
-    for copy in loads[4:]:
-        copy.wait()
     take_down(0)
     peer_half(0)
     expert(0, rows, gate_y, up_y, units, 1)

time: 107 us -> 107 us (level)
  no operation moved by 1% of the time
where the time goes in v10:
time: 107 us
  Pallas kernels  105 us (98%)
  between operations  1.29 us (1%)
    pallas_call x1, Pallas kernels, split_step(): pl.pallas_call(functools.partial(split_kernel, factor, replicas), in_spec...  102 us
    pallas_call x1, Pallas kernels, store_step(): pl.pallas_call(store_kernel, in_specs=[vmem] * 2, out_specs=[hbm] * 2, ou...  2.99 us

profile of v10, /device:TPU:0, one launch (start us, length us, event | category | flops | bytes accessed | tf_op | source)
XLA Modules:
  0.0 106.6 jit_solution(11112936785302013963)
XLA Ops:
  1.3 102.3 %split_step.1 = (f32[1,512,2304]{2,1,0:T(8,128)S(1)}, bf16[512,2304]{1,0:T(8,128)(2,1)S(1)}) custom-call(bf16[256,2304]{1,0:T(8,128)(2,1)} %tokens_hbm.1, bf16[256,2304]{1,0:T(8,128)(2,1)} %target_hbm.1, bf16[256]{0:T(256)(128)(2,1)} %combine_hbm.1, s32[1]{0:T(128)S(6)} %copy.18.filled, bf16[2304,512]{1,0:T(8,128)(2,1)} %gate_hbm.1, ...), custom_call_target="tpu_custom_call" | custom-call | tf_op jit(solution)/shard_map/split_step/pallas_call | solution.py:559
  103.6 3.0 %store_step.1 = (f32[1,512,2304]{2,1,0:T(8,128)}, bf16[512,2304]{1,0:T(8,128)(2,1)}) custom-call(f32[1,512,2304]{2,1,0:T(8,128)S(1)} %get-tuple-element.4.state, bf16[512,2304]{1,0:T(8,128)(2,1)S(1)} %get-tuple-element.5.update), custom_call_target="tpu_custom_call" | custom-call | tf_op jit(solution)/shard_map/store_step/pallas_call | solution.py:538
